TPU v7x, 128 devices: a whole 4x4x4 slice. The times are simulated.
128 devices in a mesh: scen: 8 (over z_lo, x), opt: 16 (over z_hi, y, core).
Axes of the slice: x: 4, y: 4, z: 4 (z_hi: 2, z_lo: 2; z = z_hi * 2 + z_lo), core: 2. Of those that a mesh axis runs over, the one named last changes fastest.
Arguments:
- option_coefs: float32 [16384, 1024], P(('opt', 'scen')), may hold values from -0.75 to 0.75
- underlying_of: int32 [16384, 1], P('opt'), may hold values from 0 to 127; in each aligned block of 128 rows (0 to 127, 128 to 255, ...) at most 2 rows name the same one
- log_return_mean: float32 [128, 2048], P(('scen', 'opt')), may hold values from -1 to 1
- log_return_spread: float32 [128, 2048], P(('scen', 'opt')), may hold values from 1e-06 to 0.0001
- cost: float32 [16384], P('opt'), may hold values from -3 to 3
- positions: float32 [16384], P('opt'), may hold values from -1 to 1
- base_loss: float32 [2048], P('scen'), may hold values from -6 to 6
- duals: float32 [2048], P('scen'), may hold values from 0 to 1
- threshold: float32 [1], replicated, may hold values from -2 to 2
Outputs:
- scenario_values: float32 [16384, 2048], P('opt', 'scen')
- new_positions: float32 [16384], P('opt')
- new_duals: float32 [2048], P('scen')
- new_threshold: float32 [1], replicated
Inputs may be any that keep to these rules, and one draw needn't show every extreme that they name: `underlying_of`: in each aligned block of 128 options no underlying is named more than 2 times, a bound that some block reaches; every underlying is named somewhere.
All inputs are finite; a program needn't handle non-finite values.
Results may differ from a plain program's by a relative error of at most 0.0003.
Values sent between devices are 32-bit elements; how exact they have to be, the bound alone decides.
No kernel may reach another device: no remote copies, remote signals or barrier semaphores. Data moves between devices by JAX's collectives and lax.ppermute only.
A program may use at most 64 MiB of HBM per device.

v0:
```python
import math

import jax
import jax.numpy as jnp
from jax import lax
from jax.sharding import PartitionSpec as P

ITERS = 2


LOW_END = -4.0
HIGH_END = 4.0
TAIL_LEVEL = 0.9
PRIMAL_STEP = 0.5
THRESH_STEP = 0.05
DUAL_STEP = 0.5


def sent_to_all(shard, axis):
    copies = jnp.broadcast_to(shard, (lax.axis_size(axis), *shard.shape))
    return lax.all_to_all(copies, axis, split_axis=0, concat_axis=0, tiled=True)


def over_copies(shard, axis):
    everything = sent_to_all(shard, axis)
    return jnp.sum(everything, axis=0)


def together(arrays, axis):
    vector, at, done = (jnp.concatenate([a.reshape(-1) for a in arrays]), 0, [])
    running = over_copies(vector, axis)
    for a in arrays:
        done.append(running[at : at + a.size].reshape(a.shape))
        at += a.size
    return tuple(done)


def cosine_terms(drift_rows, variance_rows, term_count):
    frequency = jnp.arange(term_count, dtype=jnp.float32) * (math.pi / (HIGH_END - LOW_END))
    weight = jnp.where(jnp.arange(term_count) == 0, 0.5, 1.0).astype(jnp.float32) * (
        2.0 / (HIGH_END - LOW_END)
    )
    decay = jnp.exp(-0.5 * variance_rows[:, None] * frequency * frequency)
    return weight * decay * jnp.cos(frequency * (drift_rows[:, None] - LOW_END))


def slot_ranks(owners, label_count):
    onehot = (owners[..., None] == jnp.arange(label_count, dtype=jnp.int32)).astype(jnp.int32)
    before = jnp.cumsum(onehot, axis=1) - onehot
    return jnp.sum(before * onehot, axis=-1)


def on_device(
    option_coefs,
    underlying_of,
    log_return_mean,
    log_return_spread,
    cost,
    positions,
    base_loss,
    duals,
    threshold,
):
    outcome_total = lax.axis_size("scen")
    opt_count = lax.axis_size("opt")
    processor_total = outcome_total * opt_count
    my_row = lax.axis_index("scen")
    block_rows = option_coefs.shape[0]
    term_count = option_coefs.shape[1]
    outcome_lines = duals.shape[0]
    total_scen = log_return_mean.shape[1]
    place_limit = max(2, 2 * block_rows // processor_total)
    column_owner = underlying_of[:, 0].reshape(outcome_total, block_rows)
    column_rank = slot_ranks(column_owner, processor_total)
    my_owner = lax.dynamic_index_in_dim(column_owner, my_row, 0, keepdims=False)
    my_rank = lax.dynamic_index_in_dim(column_rank, my_row, 0, keepdims=False)
    outgoing = jnp.zeros((processor_total * place_limit, term_count), jnp.float32)
    outgoing = outgoing.at[my_owner * place_limit + my_rank].set(option_coefs)
    incoming = lax.all_to_all(
        outgoing.reshape(processor_total, place_limit, term_count),
        ("scen", "opt"),
        split_axis=0,
        concat_axis=0,
        tiled=True,
    )
    incoming = incoming.reshape(outcome_total, opt_count, place_limit, term_count)
    contraction = "abmk,sk->bams"
    holding_buffer_dims = (outcome_total, opt_count, outcome_total, place_limit, outcome_lines)

    def contract_cost_tile(cost_tile_number, valued_contracts):
        drift_rows = lax.dynamic_slice_in_dim(
            log_return_mean[0], cost_tile_number * outcome_lines, outcome_lines
        )
        variance_rows = lax.dynamic_slice_in_dim(
            log_return_spread[0], cost_tile_number * outcome_lines, outcome_lines
        )
        cosine_table = cosine_terms(drift_rows, variance_rows, term_count)
        contract_worths = jnp.einsum(
            contraction, incoming, cosine_table, precision=lax.Precision.HIGHEST
        )
        return lax.dynamic_update_index_in_dim(
            valued_contracts, contract_worths, cost_tile_number, 0
        )

    valued_contracts = lax.fori_loop(
        0, outcome_total, contract_cost_tile, jnp.zeros(holding_buffer_dims, jnp.float32)
    )
    arrived = lax.all_to_all(
        valued_contracts.reshape(processor_total, outcome_total, place_limit, outcome_lines),
        ("scen", "opt"),
        split_axis=0,
        concat_axis=0,
        tiled=True,
    )
    flat_index = (
        column_owner * outcome_total + jnp.arange(outcome_total, dtype=jnp.int32)[:, None]
    ) * place_limit + column_rank
    local_tile = jnp.take(
        arrived.reshape(processor_total * outcome_total * place_limit, outcome_lines),
        flat_index.reshape(-1),
        axis=0,
    )
    root_scen = math.sqrt(total_scen)
    root_opt = math.sqrt(opt_count * local_tile.shape[0])
    tail_mass = (1.0 - TAIL_LEVEL) * total_scen
    holding = positions
    weights = duals
    level = threshold[0]
    for iteration in range(ITERS):
        part_gradient = jnp.dot(local_tile, weights, precision=lax.Precision.HIGHEST)
        gradient_sum, dual_mass = together((part_gradient, jnp.sum(weights)), "scen")
        holding_next = jnp.clip(
            holding - PRIMAL_STEP * (cost - gradient_sum / root_scen), -1.0, 1.0
        )
        level_next = level - THRESH_STEP * (1.0 - dual_mass / tail_mass)
        holding_bar = 2.0 * holding_next - holding
        level_bar = 2.0 * level_next - level
        part_pnl = jnp.dot(holding_bar, local_tile, precision=lax.Precision.HIGHEST)
        pnl = over_copies(part_pnl, "opt") / root_opt
        weights = jnp.clip(weights + DUAL_STEP * (base_loss - pnl - level_bar), 0.0, 1.0)
        holding = holding_next
        level = level_next
    return (local_tile, holding, weights, level.reshape(1))


def solution(mesh):
    in_specs = (
        P(("opt", "scen"), None),
        P("opt", None),
        P(("scen", "opt"), None),
        P(("scen", "opt"), None),
        P("opt"),
        P("opt"),
        P("scen"),
        P("scen"),
        P(),
    )
    out_specs = (P("opt", "scen"), P("opt"), P("scen"), P())
    return jax.shard_map(
        on_device, mesh=mesh, in_specs=in_specs, out_specs=out_specs, check_vma=False
    )
```

profile of v0, /device:TPU:1, one launch (start us, length us, event | category | flops | bytes accessed | tf_op | source)
XLA Modules:
  0.0 181.8 jit_solution(7010368312084052745)
XLA Ops:
  1.4 2.5 %select_reduce_fusion = s32[8,128]{0,1:T(8,128)S(1)} fusion(s32[8,128]{0,1:T(8,128)S(1)} %copy.37), kind=kOutput, calls=%fused_computation.27 | output fusion | flops 17562624 | bytes 8192 | tf_op jit(solution)/shard_map/jit(cumsum)/reduce_window_sum | solution.py:49
  4.1 1.8 scatter_custom_fusion
  7.5 11.5 %all-to-all-start = ((f32[128,2,1024]{2,1,0:T(2,128)}), f32[128,2,1024]{2,1,0:T(2,128)S(1)}, u32[]{:S(2)}, u32[]{:S(2)}) async-start(f32[128,2,1024]{2,1,0:T(2,128)} %reshape.146), calls=%async_computation | async-start | bytes 2097152 | tf_op jit(solution)/shard_map/all_to_all | solution.py:79
  19.0 18.9 %all-to-all-done = f32[128,2,1024]{2,1,0:T(2,128)S(1)} async-done(((f32[128,2,1024]{2,1,0:T(2,128)}), f32[128,2,1024]{2,1,0:T(2,128)S(1)}, u32[]{:S(2)}, u32[]{:S(2)}) %all-to-all-start) | async-done | bytes 1048608 | tf_op jit(solution)/shard_map/all_to_all | solution.py:79
  38.3 50.2 %while.15 = (s32[]{:T(128)}, f32[8,16,8,2,256]{4,2,3,1,0:T(8,128)}, f32[1,2048]{1,0:T(1,128)}, f32[1,2048]{1,0:T(1,128)}, f32[8,16,2,1024]{3,1,2,0:T(8,128)S(1)}...) while((s32[]{:T(128)}, f32[8,16,8,2,256]{4,2,3,1,0:T(8,128)}, f32[1,2048]{1,0:T(1,128)}, ...), condition=%wide.region_4.5_spmd, body=%wide.region_3.4_spmd.sunk | while | flops 806621696 | bytes 1857691 | solution.py:105
  39.0 4.7 %convolution_bitcast_fusion.2 = f32[1,16,8,2,256]{4,1,3,2,0:T(8,128)S(1)} fusion(f32[8,16,2,1024]{3,1,2,0:T(8,128)S(1)} %get-tuple-element.243, f32[256]{0:T(256)S(1)} %bitcast.58, f32[1024]{0:T(1024)S(1)} %get-tuple-element.218, f32[256]{0:T(256)S(1)} %bitcast.59, f32[1024]{0:T(1024)S(1)} %get-tuple-element.220), kind=kOutput, calls=%fused_computation.2.clone.1 | convolution fusion | flops 806617088 | bytes 1320960 | tf_op jit(solution)/shard_map/while/body/eval_jaxpr/abmk,sk->bams/dot_general | solution.py:98
  45.3 4.7 %convolution_bitcast_fusion.2 = f32[1,16,8,2,256]{4,1,3,2,0:T(8,128)S(1)} fusion(f32[8,16,2,1024]{3,1,2,0:T(8,128)S(1)} %get-tuple-element.243, f32[256]{0:T(256)S(1)} %bitcast.58, f32[1024]{0:T(1024)S(1)} %get-tuple-element.218, f32[256]{0:T(256)S(1)} %bitcast.59, f32[1024]{0:T(1024)S(1)} %get-tuple-element.220), kind=kOutput, calls=%fused_computation.2.clone.1 | convolution fusion | flops 806617088 | bytes 1320960 | tf_op jit(solution)/shard_map/while/body/eval_jaxpr/abmk,sk->bams/dot_general | solution.py:98
  51.5 4.7 %convolution_bitcast_fusion.2 = f32[1,16,8,2,256]{4,1,3,2,0:T(8,128)S(1)} fusion(f32[8,16,2,1024]{3,1,2,0:T(8,128)S(1)} %get-tuple-element.243, f32[256]{0:T(256)S(1)} %bitcast.58, f32[1024]{0:T(1024)S(1)} %get-tuple-element.218, f32[256]{0:T(256)S(1)} %bitcast.59, f32[1024]{0:T(1024)S(1)} %get-tuple-element.220), kind=kOutput, calls=%fused_computation.2.clone.1 | convolution fusion | flops 806617088 | bytes 1320960 | tf_op jit(solution)/shard_map/while/body/eval_jaxpr/abmk,sk->bams/dot_general | solution.py:98
  57.8 4.7 %convolution_bitcast_fusion.2 = f32[1,16,8,2,256]{4,1,3,2,0:T(8,128)S(1)} fusion(f32[8,16,2,1024]{3,1,2,0:T(8,128)S(1)} %get-tuple-element.243, f32[256]{0:T(256)S(1)} %bitcast.58, f32[1024]{0:T(1024)S(1)} %get-tuple-element.218, f32[256]{0:T(256)S(1)} %bitcast.59, f32[1024]{0:T(1024)S(1)} %get-tuple-element.220), kind=kOutput, calls=%fused_computation.2.clone.1 | convolution fusion | flops 806617088 | bytes 1320960 | tf_op jit(solution)/shard_map/while/body/eval_jaxpr/abmk,sk->bams/dot_general | solution.py:98
  64.1 4.7 %convolution_bitcast_fusion.2 = f32[1,16,8,2,256]{4,1,3,2,0:T(8,128)S(1)} fusion(f32[8,16,2,1024]{3,1,2,0:T(8,128)S(1)} %get-tuple-element.243, f32[256]{0:T(256)S(1)} %bitcast.58, f32[1024]{0:T(1024)S(1)} %get-tuple-element.218, f32[256]{0:T(256)S(1)} %bitcast.59, f32[1024]{0:T(1024)S(1)} %get-tuple-element.220), kind=kOutput, calls=%fused_computation.2.clone.1 | convolution fusion | flops 806617088 | bytes 1320960 | tf_op jit(solution)/shard_map/while/body/eval_jaxpr/abmk,sk->bams/dot_general | solution.py:98
  70.3 4.7 %convolution_bitcast_fusion.2 = f32[1,16,8,2,256]{4,1,3,2,0:T(8,128)S(1)} fusion(f32[8,16,2,1024]{3,1,2,0:T(8,128)S(1)} %get-tuple-element.243, f32[256]{0:T(256)S(1)} %bitcast.58, f32[1024]{0:T(1024)S(1)} %get-tuple-element.218, f32[256]{0:T(256)S(1)} %bitcast.59, f32[1024]{0:T(1024)S(1)} %get-tuple-element.220), kind=kOutput, calls=%fused_computation.2.clone.1 | convolution fusion | flops 806617088 | bytes 1320960 | tf_op jit(solution)/shard_map/while/body/eval_jaxpr/abmk,sk->bams/dot_general | solution.py:98
  76.6 4.7 %convolution_bitcast_fusion.2 = f32[1,16,8,2,256]{4,1,3,2,0:T(8,128)S(1)} fusion(f32[8,16,2,1024]{3,1,2,0:T(8,128)S(1)} %get-tuple-element.243, f32[256]{0:T(256)S(1)} %bitcast.58, f32[1024]{0:T(1024)S(1)} %get-tuple-element.218, f32[256]{0:T(256)S(1)} %bitcast.59, f32[1024]{0:T(1024)S(1)} %get-tuple-element.220), kind=kOutput, calls=%fused_computation.2.clone.1 | convolution fusion | flops 806617088 | bytes 1320960 | tf_op jit(solution)/shard_map/while/body/eval_jaxpr/abmk,sk->bams/dot_general | solution.py:98
  82.9 4.7 %convolution_bitcast_fusion.2 = f32[1,16,8,2,256]{4,1,3,2,0:T(8,128)S(1)} fusion(f32[8,16,2,1024]{3,1,2,0:T(8,128)S(1)} %get-tuple-element.243, f32[256]{0:T(256)S(1)} %bitcast.58, f32[1024]{0:T(1024)S(1)} %get-tuple-element.218, f32[256]{0:T(256)S(1)} %bitcast.59, f32[1024]{0:T(1024)S(1)} %get-tuple-element.220), kind=kOutput, calls=%fused_computation.2.clone.1 | convolution fusion | flops 806617088 | bytes 1320960 | tf_op jit(solution)/shard_map/while/body/eval_jaxpr/abmk,sk->bams/dot_general | solution.py:98
  88.5 4.7 %all-to-all-start.1 = ((f32[128,8,2,256]{3,1,2,0:T(8,128)}), f32[128,8,2,256]{3,1,2,0:T(8,128)S(1)}, u32[]{:S(2)}, u32[]{:S(2)}) async-start(f32[128,8,2,256]{3,1,2,0:T(8,128)} %bitcast.11), calls=%async_computation.1 | async-start | bytes 4194304 | tf_op jit(solution)/shard_map/all_to_all | solution.py:108
  93.8 30.6 %all-to-all-done.1 = f32[128,8,2,256]{3,1,2,0:T(8,128)S(1)} async-done(((f32[128,8,2,256]{3,1,2,0:T(8,128)}), f32[128,8,2,256]{3,1,2,0:T(8,128)S(1)}, u32[]{:S(2)}, u32[]{:S(2)}) %all-to-all-start.1) | async-done | bytes 2097184 | tf_op jit(solution)/shard_map/all_to_all | solution.py:108
  124.5 2.4 %copy.43 = f32[128,8,2,256]{3,2,1,0:T(2,128)} copy(f32[128,8,2,256]{3,1,2,0:T(8,128)S(1)} %all-to-all-done.1) | data formatting | bytes 4194304 | tf_op jit(solution)/shard_map/all_to_all | solution.py:108
  126.9 2.7 %reshape.149 = f32[2048,256]{1,0:T(8,128)S(1)} reshape(f32[128,8,2,256]{3,2,1,0:T(2,128)} %copy.43) | data formatting | bytes 4194304 | tf_op jit(solution)/shard_map/reshape | solution.py:119
  129.6 3.5 %gather_fusion = f32[1024,256]{1,0:T(8,128)S(1)} fusion(f32[2048,256]{1,0:T(8,128)S(1)} %reshape.149, s32[1024]{0:T(1024)S(1)} %broadcast_clamp_fusion), kind=kCustom, calls=%fused_computation | custom fusion | bytes 2101248 | tf_op jit(solution)/shard_map/jit(_take)/gather | solution.py:118
  135.0 7.5 %all_to_all.34 = f32[8,1,1025]{2,1,0:T(1,128)S(1)} all-to-all(f32[8,1,1025]{2,1,0:T(1,128)S(1)} %broadcast_in_dim.72), channel_id=1, replica_groups=mesh['scen'=8,'opt'=16] {'scen'}, dimensions={0} | all-to-all | bytes 65600 | tf_op jit(solution)/shard_map/all_to_all | solution.py:21
  143.7 5.2 %all-to-all-start.3 = ((f32[16,1,256]{2,1,0:T(1,128)}), f32[16,1,256]{2,1,0:T(1,128)S(1)}, u32[]{:S(2)}, u32[]{:S(2)}) async-start(f32[16,1,256]{2,1,0:T(1,128)} %broadcast_in_dim.73), calls=%async_computation.3 | async-start | bytes 32768 | tf_op jit(solution)/shard_map/all_to_all | solution.py:21
  150.8 5.5 %all-to-all-done.3 = f32[16,1,256]{2,1,0:T(1,128)S(1)} async-done(((f32[16,1,256]{2,1,0:T(1,128)}), f32[16,1,256]{2,1,0:T(1,128)S(1)}, u32[]{:S(2)}, u32[]{:S(2)}) %all-to-all-start.3) | async-done | bytes 16416 | tf_op jit(solution)/shard_map/all_to_all | solution.py:21
  158.6 7.5 %all_to_all.35 = f32[8,1,1025]{2,1,0:T(1,128)S(1)} all-to-all(f32[8,1,1025]{2,1,0:T(1,128)S(1)} %broadcast_in_dim.74), channel_id=1, replica_groups=mesh['scen'=8,'opt'=16] {'scen'}, dimensions={0} | all-to-all | bytes 65600 | tf_op jit(solution)/shard_map/all_to_all | solution.py:21
  167.9 4.8 %all-to-all-start.5 = ((f32[16,1,256]{2,1,0:T(1,128)}), f32[16,1,256]{2,1,0:T(1,128)S(1)}, u32[]{:S(2)}, u32[]{:S(2)}) async-start(f32[16,1,256]{2,1,0:T(1,128)} %broadcast_in_dim.75), calls=%async_computation.5 | async-start | bytes 32768 | tf_op jit(solution)/shard_map/all_to_all | solution.py:21
  173.9 6.2 %all-to-all-done.5 = f32[16,1,256]{2,1,0:T(1,128)S(1)} async-done(((f32[16,1,256]{2,1,0:T(1,128)}), f32[16,1,256]{2,1,0:T(1,128)S(1)}, u32[]{:S(2)}, u32[]{:S(2)}) %all-to-all-start.5) | async-done | bytes 16416 | tf_op jit(solution)/shard_map/all_to_all | solution.py:21
  (68 shorter events, 25.0 us)
Async XLA Ops:
  7.5 30.4 %all-to-all-start = ((f32[128,2,1024]{2,1,0:T(2,128)}), f32[128,2,1024]{2,1,0:T(2,128)S(1)}, u32[]{:S(2)}, u32[]{:S(2)}) async-start(f32[128,2,1024]{2,1,0:T(2,128)} %reshape.146), calls=%async_computation | async-start | bytes 2097152 | tf_op jit(solution)/shard_map/all_to_all | solution.py:79
  88.5 4.7 %copy-start.4 = (f32[256]{0:T(256)S(1)}, f32[256]{0:T(256)}, u32[]{:S(2)}) copy-start(f32[256]{0:T(256)} %param.18) | copy-start | bytes 3076
  88.5 5.3 %copy-start.1 = (s32[1024,1]{0,1:T(1,128)S(1)}, s32[1024,1]{0,1:T(1,128)}, u32[]{:S(2)}) copy-start(s32[1024,1]{0,1:T(1,128)} %param.12) | copy-start | bytes 12292
  88.5 36.0 %all-to-all-start.1 = ((f32[128,8,2,256]{3,1,2,0:T(8,128)}), f32[128,8,2,256]{3,1,2,0:T(8,128)S(1)}, u32[]{:S(2)}, u32[]{:S(2)}) async-start(f32[128,8,2,256]{3,1,2,0:T(8,128)} %bitcast.11), calls=%async_computation.1 | async-start | bytes 4194304 | tf_op jit(solution)/shard_map/all_to_all | solution.py:108
  133.1 9.5 %copy-start.2 = (f32[1024]{0:T(1024)S(1)}, f32[1024]{0:T(1024)}, u32[]{:S(2)}) copy-start(f32[1024]{0:T(1024)} %param.16) | copy-start | bytes 12292
  133.1 9.5 %copy-start.3 = (f32[1024]{0:T(1024)S(1)}, f32[1024]{0:T(1024)}, u32[]{:S(2)}) copy-start(f32[1024]{0:T(1024)} %param.15) | copy-start | bytes 12292
  133.1 23.2 %copy-start.5 = (f32[256]{0:T(256)S(1)}, f32[256]{0:T(256)}, u32[]{:S(2)}) copy-start(f32[256]{0:T(256)} %param.17) | copy-start | bytes 3076
  133.3 33.9 %copy-start = (f32[1024,256]{1,0:T(8,128)}, f32[1024,256]{1,0:T(8,128)S(1)}, u32[]{:S(2)}) copy-start(f32[1024,256]{1,0:T(8,128)S(1)} %broadcast_select_fusion) | copy-start | bytes 3145732
  143.7 12.5 %all-to-all-start.3 = ((f32[16,1,256]{2,1,0:T(1,128)}), f32[16,1,256]{2,1,0:T(1,128)S(1)}, u32[]{:S(2)}, u32[]{:S(2)}) async-start(f32[16,1,256]{2,1,0:T(1,128)} %broadcast_in_dim.73), calls=%async_computation.3 | async-start | bytes 32768 | tf_op jit(solution)/shard_map/all_to_all | solution.py:21
  167.9 12.2 %all-to-all-start.5 = ((f32[16,1,256]{2,1,0:T(1,128)}), f32[16,1,256]{2,1,0:T(1,128)S(1)}, u32[]{:S(2)}, u32[]{:S(2)}) async-start(f32[16,1,256]{2,1,0:T(1,128)} %broadcast_in_dim.75), calls=%async_computation.5 | async-start | bytes 32768 | tf_op jit(solution)/shard_map/all_to_all | solution.py:21
where the time goes:
time: 183 us; the launch traced here: 182 us
  waiting for transfers between devices  61.2 us (33%)
  matrix products  40.5 us (22%)
  starting transfers between devices  26.2 us (14%)
  local copies, waits for them, and re-layouts  22.4 us (12%)
  blocking collectives  15 us (8%)
  other arithmetic  12.5 us (7%)
  between operations  3.92 us (2%)
    dot_general x8, matrix products, contract_cost_tile(): jnp.einsum(contraction, incoming, cosine_table, precision=lax.Precision.H...  37.5 us
    all_to_all x1, waiting for transfers between devices, on_device(): lax.all_to_all(valued_contracts.reshape(processor_total, outcome_total, p...  30.6 us
    all_to_all x1, waiting for transfers between devices, on_device(): lax.all_to_all(outgoing.reshape(processor_total, place_limit, term_count)...  18.9 us
    all_to_all x2, blocking collectives, sent_to_all(): return lax.all_to_all(copies, axis, split_axis=0, concat_axis=0, tiled=True)  15 us
    all_to_all x2, waiting for transfers between devices, sent_to_all(): return lax.all_to_all(copies, axis, split_axis=0, concat_axis=0, tiled=True)  11.6 us
    all_to_all x1, starting transfers between devices, on_device(): lax.all_to_all(outgoing.reshape(processor_total, place_limit, term_count)...  11.5 us
    all_to_all x2, starting transfers between devices, sent_to_all(): return lax.all_to_all(copies, axis, split_axis=0, concat_axis=0, tiled=True)  10.1 us
    dynamic_update_slice x8, local copies, waits for them, and re-layouts, contract_cost_tile(): lax.dynamic_update_index_in_dim(valued_contracts, contract_worths, cost_t...  6.95 us
  transfers between devices with their start and end apart: 4, of which 4 were waited for; matrix products, arithmetic and copies ran while one was open for 1% of the time, Pallas kernels for 0%

commit v1 on v0

v1 whole, which is shorter than its diff:
```python
import math

import jax
import jax.numpy as jnp
from jax import lax
from jax.experimental import pallas as pl
from jax.experimental.pallas import tpu as pltpu
from jax.sharding import PartitionSpec as P

LOW_END = -4.0
HIGH_END = 4.0
TAIL_LEVEL = 0.9
PRIMAL_STEP = 0.5
THRESH_STEP = 0.05
DUAL_STEP = 0.5

LANES = 128
SCEN = 8
OPT = 16
DEVICES = SCEN * OPT
TERMS = 1024
SCENARIOS = 2048
OPTIONS = 16384
MOST = 2
CHUNKS = TERMS // LANES
BASE = 32
COEF_ROWS = CHUNKS + 1
MSG1 = MOST * COEF_ROWS + 2
MSG2 = MOST * 16 + 2
PAYLOAD = 24
ORDER = ("opt", "scen")
F32 = jnp.float32
BF16 = jnp.bfloat16
HIGHEST = lax.Precision.HIGHEST
NN = (((1,), (0,)), ((), ()))
NT = (((1,), (1,)), ((), ()))


def params():
    return pltpu.CompilerParams(vmem_limit_bytes=48 * 1024 * 1024)


def iota(shape, axis):
    return lax.broadcasted_iota(jnp.int32, shape, axis)


def owner_of(place):
    return (place & (SCEN - 1)) * OPT + (place >> 3)


def mm(a, b, dims=NN):
    return lax.dot_general(a, b, dims, preferred_element_type=F32)


def three(x):
    hi = x.astype(BF16)
    rest = x - hi.astype(F32)
    mid = rest.astype(BF16)
    low = (rest - mid.astype(F32)).astype(BF16)
    return hi, mid, low


def pick(onehot, x, dims=NN):
    hi, mid, low = three(x)
    return mm(onehot, hi, dims) + mm(onehot, mid, dims) + mm(onehot, low, dims)


def level_step(level, mass):
    return level - THRESH_STEP * (1.0 - mass / ((1.0 - TAIL_LEVEL) * SCENARIOS))


def primal(position, cost, gradient):
    return jnp.clip(
        position - PRIMAL_STEP * (cost - gradient / math.sqrt(SCENARIOS)), -1.0, 1.0
    )


def dual(weights, base, pnl, level_bar):
    return jnp.clip(
        weights + DUAL_STEP * (base - pnl / math.sqrt(OPTIONS) - level_bar), 0.0, 1.0
    )


def send_kernel(own_ref, coef_ref, cost_ref, pos_ref, dual_ref, out_ref):
    row = lax.axis_index("scen")
    square = (LANES, LANES)
    down, across = iota(square, 0), iota(square, 1)
    same = own_ref[pl.ds(row, 1), :] == owner_of(down)
    before = mm(
        same.astype(F32).astype(BF16), (down < across).astype(F32).astype(BF16)
    )
    cost = jnp.broadcast_to(cost_ref[pl.ds(row, 1), :], square)
    pos = jnp.broadcast_to(pos_ref[pl.ds(row, 1), :], square)
    pair = jnp.where(down == 0, cost, jnp.where(down == 1, pos, 0.0))
    for rank in range(MOST):
        chosen = jnp.where(same & (before == float(rank)), 1.0, 0.0).astype(BF16)
        for chunk in range(CHUNKS):
            out_ref[pl.ds(rank * COEF_ROWS + chunk, DEVICES, stride=MSG1), :] = pick(
                chosen, coef_ref[:, chunk * LANES : (chunk + 1) * LANES]
            )
        out_ref[pl.ds(rank * COEF_ROWS + CHUNKS, DEVICES, stride=MSG1), :] = pick(
            chosen, pair, NT
        )
    for half in range(2):
        out_ref[pl.ds(MSG1 - 2 + half, DEVICES, stride=MSG1), :] = jnp.broadcast_to(
            dual_ref[half : half + 1, :], square
        )


def turn(quarters, rest):
    x = rest * (2.0 * math.pi)
    z = x * x
    sin = x * (
        1.0 + z * (-1 / 6 + z * (1 / 120 + z * (-1 / 5040 + z * (1 / 362880))))
    )
    cos = 1.0 + z * (
        -1 / 2 + z * (1 / 24 + z * (-1 / 720 + z * (1 / 40320 - z * (1 / 3628800))))
    )
    swap = (quarters & 1) == 1
    cos_out = jnp.where(swap, sin, cos)
    sin_out = jnp.where(swap, cos, sin)
    cos_out = jnp.where(((quarters + 1) & 2) == 2, -cos_out, cos_out)
    sin_out = jnp.where((quarters & 2) == 2, -sin_out, sin_out)
    return cos_out, sin_out


def table_kernel(mean_ref, spread_ref, hi_ref, low_ref):
    width = mean_ref.shape[1]
    shape = (BASE, width)
    mean = mean_ref[...]
    coarse = jnp.round(mean * 2048.0) * (1.0 / 2048.0)
    fine = mean - coarse
    step = iota(shape, 0)
    stepf = step.astype(F32)

    def base(scale, extra):
        turns = (stepf * scale) * coarse
        quarters = jnp.round(turns * 4.0)
        rest = (turns - quarters * 0.25) + (stepf * scale) * fine
        return turn(quarters.astype(jnp.int32) + extra, rest)

    cos_b, sin_b = base(1.0 / 16.0, step)
    cos_a, sin_a = base(BASE / 16.0, jnp.zeros_like(step))
    cos_a, sin_a = cos_a * 0.25, sin_a * 0.25
    unit = math.pi / (HIGH_END - LOW_END)
    rate = spread_ref[...] * (-0.5 * unit * unit * math.log2(math.e))
    for a in range(BASE):
        k = stepf + float(BASE * a)
        decay = jnp.exp2((k * k) * rate)
        value = (cos_a[a : a + 1, :] * cos_b - sin_a[a : a + 1, :] * sin_b) * decay
        if a == 0:
            value = jnp.where(step == 0, value * 0.5, value)
        hi = value.astype(BF16)
        hi_ref[a * BASE : (a + 1) * BASE, :] = hi
        low_ref[a * BASE : (a + 1) * BASE, :] = (value - hi.astype(F32)).astype(BF16)


def value_kernel(
    in_ref, hi_ref, low_ref, out_ref, mass_ref, coef_hi, coef_low, values, grad
):
    block = pl.program_id(0)

    @pl.when(block == 0)
    def _():
        for rank in range(MOST):
            for chunk in range(CHUNKS):
                part = in_ref[pl.ds(rank * COEF_ROWS + chunk, DEVICES, stride=MSG1), :]
                hi = part.astype(BF16)
                at = (slice(rank * LANES, (rank + 1) * LANES), slice(chunk * LANES, (chunk + 1) * LANES))
                coef_hi[at] = hi
                coef_low[at] = (part - hi.astype(F32)).astype(BF16)
        grad[...] = jnp.zeros_like(grad)

    width = 2 * LANES
    table_hi = hi_ref[...]
    tile = (
        mm(coef_hi[...], table_hi)
        + mm(coef_hi[...], low_ref[...])
        + mm(coef_low[...], table_hi)
    )
    values[:, pl.ds(pl.multiple_of(block * width, width), width)] = tile
    first = in_ref[pl.ds(block * MSG1 + MSG1 - 2, 1), :]
    second = in_ref[pl.ds(block * MSG1 + MSG1 - 1, 1), :]
    grad[...] += tile[:, :LANES] * first + tile[:, LANES:] * second
    for o in range(OPT):
        for rank in range(MOST):
            for half in range(2):
                out_ref[
                    pl.ds((o * SCEN + block) * MSG2 + (rank * 2 + half) * 8, 8), :
                ] = tile[
                    rank * LANES + o * 8 : rank * LANES + o * 8 + 8,
                    half * LANES : (half + 1) * LANES,
                ]

    @pl.when(block == SCEN - 1)
    def _():
        mass = jnp.zeros((1, LANES), F32)
        for s in range(SCEN):
            for half in range(2):
                mass = mass + in_ref[s * MSG1 + MSG1 - 2 + half : s * MSG1 + MSG1 - 1 + half, :]
        mass_ref[0] = jnp.sum(mass)
        pnl = jnp.zeros((8, SCENARIOS), F32)
        for rank in range(MOST):
            extra = in_ref[pl.ds(rank * COEF_ROWS + CHUNKS, DEVICES, stride=MSG1), :]
            cost, pos = extra[:, 0:1], extra[:, 1:2]
            gradient = jnp.sum(grad[rank * LANES : (rank + 1) * LANES, :], axis=1, keepdims=True)
            bar = 2.0 * primal(pos, cost, gradient) - pos
            for group in range(LANES // 8):
                pnl = pnl + values[rank * LANES + group * 8 : rank * LANES + group * 8 + 8, :] * bar[group * 8 : group * 8 + 8, :]
        pnl = jnp.sum(pnl, axis=0, keepdims=True)
        for s in range(SCEN):
            for half in range(2):
                at = s * width + half * LANES
                out_ref[pl.ds(s * MSG2 + MSG2 - 2 + half, OPT, stride=SCEN * MSG2), :] = (
                    jnp.broadcast_to(pnl[:, at : at + LANES], (OPT, LANES))
                )


def tile_kernel(
    in_ref, own_ref, dual_ref, base_ref, mass_ref, level_ref, tile_ref, pay_ref, dual_out
):
    square = (LANES, LANES)
    down, across = iota(square, 0), iota(square, 1)
    level = level_ref[0]
    level_bar = 2.0 * level_step(level, mass_ref[0]) - level
    weights = []
    for half in range(2):
        pnl = jnp.sum(
            in_ref[pl.ds(MSG2 - 2 + half, DEVICES, stride=MSG2), :], axis=0, keepdims=True
        )
        weights.append(
            dual(dual_ref[half : half + 1, :], base_ref[half : half + 1, :], pnl, level_bar)
        )
        dual_out[half : half + 1, :] = weights[half]
    new = jnp.concatenate(weights, axis=1)
    old = jnp.concatenate([dual_ref[0:1, :], dual_ref[1:2, :]], axis=1)
    tall = iota((8, 2 * LANES), 0)
    both = jnp.where(
        tall == 0,
        jnp.broadcast_to(old, (8, 2 * LANES)),
        jnp.where(tall == 1, jnp.broadcast_to(new, (8, 2 * LANES)), 0.0),
    )
    names = jnp.concatenate([own_ref[...].astype(F32), jnp.zeros((LANES - SCEN, LANES), F32)], axis=0).T
    lower = (across < down).astype(F32).astype(BF16)
    owner = owner_of(across).astype(F32)
    rows = []
    for s in range(SCEN):
        same = names[:, s : s + 1] == owner
        before = mm(lower, same.astype(F32).astype(BF16))
        chosen = jnp.concatenate(
            [
                jnp.where(same & (before == float(rank)), 1.0, 0.0).astype(BF16)
                for rank in range(MOST)
            ],
            axis=1,
        )
        arrived = jnp.concatenate(
            [
                jnp.concatenate(
                    [
                        in_ref[pl.ds((rank * 2 + half) * 8 + s, DEVICES, stride=MSG2), :]
                        for half in range(2)
                    ],
                    axis=1,
                )
                for rank in range(MOST)
            ],
            axis=0,
        )
        tile = pick(chosen, arrived)
        tile_ref[s * LANES : (s + 1) * LANES, :] = tile
        rows.append(
            lax.dot_general(both, tile, NT, precision=HIGHEST, preferred_element_type=F32)
        )
    payload = jnp.concatenate(
        [r[0:1, :] for r in rows]
        + [r[1:2, :] for r in rows]
        + [weights[0] + weights[1], jnp.zeros((PAYLOAD - 17, LANES), F32)],
        axis=0,
    )
    for s in range(SCEN):
        pay_ref[s * PAYLOAD : (s + 1) * PAYLOAD, :] = payload


def position_kernel(
    in_ref, tile_ref, cost_ref, pos_ref, mass_ref, level_ref, pos_out, pnl_out, level_out, bar_out
):
    total = in_ref[0:PAYLOAD, :]
    for s in range(1, SCEN):
        total = total + in_ref[s * PAYLOAD : (s + 1) * PAYLOAD, :]
    level = level_step(level_ref[0], mass_ref[0])
    later = level_step(level, jnp.sum(total[16:17, :]))
    level_out[0] = later
    bar_out[0] = 2.0 * later - level
    cost = cost_ref[...]
    first = primal(pos_ref[...], cost, total[0:8, :])
    second = primal(first, cost, total[8:16, :])
    pos_out[...] = second
    bar = 2.0 * second - first
    pnl = jnp.zeros((1, 2 * LANES), F32)
    for s in range(SCEN):
        pnl = pnl + lax.dot_general(
            bar[s : s + 1, :],
            tile_ref[s * LANES : (s + 1) * LANES, :],
            NN,
            precision=HIGHEST,
            preferred_element_type=F32,
        )
    for o in range(OPT):
        for half in range(2):
            pnl_out[o * 2 + half : o * 2 + half + 1, :] = pnl[:, half * LANES : (half + 1) * LANES]


def dual_kernel(in_ref, dual_ref, base_ref, bar_ref, out_ref):
    pnl = in_ref[0:2, :]
    for o in range(1, OPT):
        pnl = pnl + in_ref[2 * o : 2 * o + 2, :]
    out_ref[...] = dual(dual_ref[...], base_ref[...], pnl, bar_ref[0])


VMEM = pl.BlockSpec(memory_space=pltpu.VMEM)
SMEM = pl.BlockSpec(memory_space=pltpu.SMEM)


def exchange(x, axes):
    return lax.all_to_all(x, axes, split_axis=0, concat_axis=0, tiled=True)


def shaped(*shape, dtype=F32):
    return jax.ShapeDtypeStruct(shape, dtype)


def on_device(
    option_coefs,
    underlying_of,
    log_return_mean,
    log_return_spread,
    cost,
    positions,
    base_loss,
    duals,
    threshold,
):
    own = underlying_of.reshape(SCEN, LANES)
    cost = cost.reshape(SCEN, LANES)
    positions = positions.reshape(SCEN, LANES)
    base_loss = base_loss.reshape(2, LANES)
    duals = duals.reshape(2, LANES)

    sent = pl.pallas_call(
        send_kernel,
        out_shape=shaped(DEVICES * MSG1, LANES),
        in_specs=[VMEM] * 5,
        out_specs=VMEM,
        compiler_params=params(),
    )(own, option_coefs, cost, positions, duals)
    got = exchange(sent.reshape(DEVICES, MSG1 // 2, 2, LANES), ORDER)
    got = got.reshape(DEVICES * MSG1, LANES)

    width = 2 * LANES
    row = pl.BlockSpec((1, width), lambda i: (0, i))
    column = pl.BlockSpec((TERMS, width), lambda i: (0, i))
    table_hi, table_low = pl.pallas_call(
        table_kernel,
        grid=(SCENARIOS // width,),
        out_shape=[shaped(TERMS, SCENARIOS, dtype=BF16)] * 2,
        in_specs=[row, row],
        out_specs=[column, column],
        compiler_params=params(),
        cost_estimate=pl.CostEstimate(
            flops=20 * TERMS * SCENARIOS,
            bytes_accessed=4 * TERMS * SCENARIOS,
            transcendentals=TERMS * SCENARIOS,
        ),
    )(log_return_mean, log_return_spread)

    whole = lambda rows: pl.BlockSpec((rows, LANES), lambda i: (0, 0))
    values, mass = pl.pallas_call(
        value_kernel,
        grid=(SCENARIOS // width,),
        out_shape=[shaped(DEVICES * MSG2, LANES), shaped(1)],
        in_specs=[whole(DEVICES * MSG1), column, column],
        out_specs=[whole(DEVICES * MSG2), SMEM],
        scratch_shapes=[
            pltpu.VMEM((MOST * LANES, TERMS), BF16),
            pltpu.VMEM((MOST * LANES, TERMS), BF16),
            pltpu.VMEM((MOST * LANES, SCENARIOS), F32),
            pltpu.VMEM((MOST * LANES, LANES), F32),
        ],
        compiler_params=params(),
    )(got, table_hi, table_low)
    arrived = exchange(values.reshape(DEVICES, MSG2 // 2, 2, LANES), ORDER)
    arrived = arrived.reshape(DEVICES * MSG2, LANES)

    tile, payload, first_duals = pl.pallas_call(
        tile_kernel,
        out_shape=[
            shaped(SCEN * LANES, width),
            shaped(SCEN * PAYLOAD, LANES),
            shaped(2, LANES),
        ],
        in_specs=[VMEM] * 4 + [SMEM] * 2,
        out_specs=[VMEM] * 3,
        compiler_params=params(),
    )(arrived, own, duals, base_loss, mass, threshold)
    gathered = exchange(payload.reshape(SCEN, PAYLOAD, LANES), "scen")

    new_positions, part_pnl, level, level_bar = pl.pallas_call(
        position_kernel,
        out_shape=[shaped(SCEN, LANES), shaped(OPT * 2, LANES), shaped(1), shaped(1)],
        in_specs=[VMEM] * 4 + [SMEM] * 2,
        out_specs=[VMEM] * 2 + [SMEM] * 2,
        compiler_params=params(),
    )(gathered.reshape(SCEN * PAYLOAD, LANES), tile, cost, positions, mass, threshold)
    pnl = exchange(part_pnl.reshape(OPT, 2, LANES), "opt")

    new_duals = pl.pallas_call(
        dual_kernel,
        out_shape=shaped(2, LANES),
        in_specs=[VMEM] * 3 + [SMEM],
        out_specs=VMEM,
        compiler_params=params(),
    )(pnl.reshape(OPT * 2, LANES), first_duals, base_loss, level_bar)
    return (tile, new_positions.reshape(-1), new_duals.reshape(-1), level)


def solution(mesh):
    in_specs = (
        P(("opt", "scen"), None),
        P("opt", None),
        P(("scen", "opt"), None),
        P(("scen", "opt"), None),
        P("opt"),
        P("opt"),
        P("scen"),
        P("scen"),
        P(),
    )
    out_specs = (P("opt", "scen"), P("opt"), P("scen"), P())
    return jax.shard_map(
        on_device, mesh=mesh, in_specs=in_specs, out_specs=out_specs, check_vma=False
    )
```

time: 183 us -> 116 us (0.63)
  matrix products: 40.5 us -> 0 us
  Pallas kernels: 0 us -> 24.4 us
  waiting for transfers between devices: 61.2 us -> 43.1 us
  local copies, waits for them, and re-layouts: 22.4 us -> 8.42 us
  other arithmetic: 12.5 us -> 0 us
  starting transfers between devices: 26.2 us -> 16.5 us
  blocking collectives: 15 us -> 21.3 us
  between operations: 3.92 us -> 1.39 us
    dot_general x12 -> x0, matrix products: 40.5 us -> none  [the longest x8 37.5 us: contract_cost_tile(): jnp.einsum(contraction, incoming, cosine_table, precision=lax.Precision.H...]
    pallas_call x0 -> x6, Pallas kernels: none -> 24.4 us  [the longest x1 9.31 us: on_device(): pl.pallas_call(value_kernel, grid=(SCENARIOS // width,), out_shape=[shape...]
    all_to_all x4 -> x2, waiting for transfers between devices: 61.2 us -> 43.1 us  [exchange(): return lax.all_to_all(x, axes, split_axis=0, concat_axis=0, tiled=True)]
    all_to_all x4 -> x2, starting transfers between devices: 26.2 us -> 16.5 us  [exchange(): return lax.all_to_all(x, axes, split_axis=0, concat_axis=0, tiled=True)]
    unnamed x12 -> x30, local copies, waits for them, and re-layouts: 0.03 us -> 8.42 us
    dynamic_update_slice x8 -> x0, local copies, waits for them, and re-layouts: 6.95 us -> none  [contract_cost_tile(): lax.dynamic_update_index_in_dim(valued_contracts, contract_worths, cost_t...]
    all_to_all x2, blocking collectives: 15 us -> 21.3 us  [exchange(): return lax.all_to_all(x, axes, split_axis=0, concat_axis=0, tiled=True)]
    sub x10 -> x0, other arithmetic: 6.2 us -> none  [the longest x8 5.59 us: cosine_terms(): return weight * decay * jnp.cos(frequency * (drift_rows[:, None] - LOW_END))]
  transfers between devices with their start and end apart: 4 -> 2, of which waited for: 4 -> 2; matrix products, arithmetic and copies ran while one was open for 1% -> 0% of each run, Pallas kernels for 0% -> 5%
where the time goes in v1:
time: 116 us; the launch traced here: 115 us
  waiting for transfers between devices  43.1 us (37%)
  Pallas kernels  24.4 us (21%)
  blocking collectives  21.3 us (18%)
  starting transfers between devices  16.5 us (14%)
  local copies, waits for them, and re-layouts  8.42 us (7%)
  between operations  1.39 us (1%)
    all_to_all x2, waiting for transfers between devices, exchange(): return lax.all_to_all(x, axes, split_axis=0, concat_axis=0, tiled=True)  43.1 us
    all_to_all x2, blocking collectives, exchange(): return lax.all_to_all(x, axes, split_axis=0, concat_axis=0, tiled=True)  21.3 us
    all_to_all x2, starting transfers between devices, exchange(): return lax.all_to_all(x, axes, split_axis=0, concat_axis=0, tiled=True)  16.5 us
    pallas_call x1, Pallas kernels, on_device(): pl.pallas_call(value_kernel, grid=(SCENARIOS // width,), out_shape=[shape...  9.31 us
    unnamed x30, local copies, waits for them, and re-layouts  8.42 us
    pallas_call x1, Pallas kernels, on_device(): pl.pallas_call(table_kernel, grid=(SCENARIOS // width,), out_shape=[shape...  6.15 us
    pallas_call x1, Pallas kernels, on_device(): pl.pallas_call(tile_kernel, out_shape=[shaped(SCEN * LANES, width), shape...  4.11 us
  transfers between devices with their start and end apart: 2, of which 2 were waited for; matrix products, arithmetic and copies ran while one was open for 0% of the time, Pallas kernels for 5%

profile of v1, /device:TPU:1, one launch (start us, length us, event | category | flops | bytes accessed | tf_op | source)
XLA Modules:
  0.0 115.2 jit_solution(12553359199130539912)
XLA Ops:
  0.6 1.0 copy-done.3
  1.7 0.7 copy-done.4
  2.4 0.7 copy-done.6
  3.1 0.7 copy-done.8
  3.7 0.7 copy-done.10
  4.4 1.9 %shard_map.120 = f32[2560,128]{1,0:T(8,128)} custom-call(s32[8,128]{1,0:T(8,128)S(1)} %bitcast.21, f32[128,1024]{1,0:T(8,128)S(1)} %copy-done.3, f32[8,128]{1,0:T(8,128)S(1)} %bitcast.23, f32[8,128]{1,0:T(8,128)S(1)} %bitcast.25, f32[2,128]{1,0:T(2,128)S(1)} %bitcast.28), custom_call_target="tpu_custom_call" | custom-call | tf_op jit(solution)/shard_map/pallas_call | solution.py:350
  6.3 11.5 %all-to-all-start = ((f32[128,10,2,128]{3,2,1,0:T(2,128)}), f32[128,10,2,128]{3,2,1,0:T(2,128)S(1)}, u32[]{:S(2)}, u32[]{:S(2)}) async-start(f32[128,10,2,128]{3,2,1,0:T(2,128)} %bitcast.4), calls=%async_computation | async-start | bytes 2621440 | tf_op jit(solution)/shard_map/all_to_all | solution.py:326
  17.9 6.1 %shard_map.121 = (bf16[1024,2048]{1,0:T(8,128)(2,1)S(1)}, bf16[1024,2048]{1,0:T(8,128)(2,1)}) custom-call(f32[1,2048]{1,0:T(1,128)S(1)} %copy-done.13, f32[1,2048]{1,0:T(1,128)S(1)} %copy-done.14), custom_call_target="tpu_custom_call" | custom-call | flops 41943040 | bytes 8388608 | tf_op jit(solution)/shard_map/pallas_call | solution.py:363
  24.0 2.0 %copy-done = bf16[1024,2048]{1,0:T(8,128)(2,1)} copy-done((bf16[1024,2048]{1,0:T(8,128)(2,1)}, bf16[1024,2048]{1,0:T(8,128)(2,1)S(1)}, u32[]{:S(2)}) %copy-start) | copy-done | bytes 4194328
  26.0 13.0 %all-to-all-done = f32[128,10,2,128]{3,2,1,0:T(2,128)S(1)} async-done(((f32[128,10,2,128]{3,2,1,0:T(2,128)}), f32[128,10,2,128]{3,2,1,0:T(2,128)S(1)}, u32[]{:S(2)}, u32[]{:S(2)}) %all-to-all-start) | async-done | bytes 1310752 | tf_op jit(solution)/shard_map/all_to_all | solution.py:326
  39.0 9.3 %shard_map.122 = (f32[4352,128]{1,0:T(8,128)S(1)}, f32[1]{0:T(128)}) custom-call(f32[2560,128]{1,0:T(8,128)S(1)} %bitcast.16, bf16[1024,2048]{1,0:T(8,128)(2,1)} %copy-done, bf16[1024,2048]{1,0:T(8,128)(2,1)} %get-tuple-element.16.low_ref), custom_call_target="tpu_custom_call" | custom-call | tf_op jit(solution)/shard_map/pallas_call | solution.py:378
  48.3 0.0 copy-start.1
  48.3 1.4 %copy-done.1 = f32[4352,128]{1,0:T(8,128)} copy-done((f32[4352,128]{1,0:T(8,128)}, f32[4352,128]{1,0:T(8,128)S(1)}, u32[]{:S(2)}) %copy-start.1) | copy-done | bytes 2228248
  49.7 5.0 %all-to-all-start.1 = ((f32[128,17,2,128]{3,2,1,0:T(2,128)}), f32[128,17,2,128]{3,2,1,0:T(2,128)S(1)}, u32[]{:S(2)}, u32[]{:S(2)}) async-start(f32[128,17,2,128]{3,2,1,0:T(2,128)} %bitcast.17), calls=%async_computation.1 | async-start | bytes 4456448 | tf_op jit(solution)/shard_map/all_to_all | solution.py:326
  54.7 0.0 copy-start.7
  54.7 0.0 copy-start.9
  55.4 30.2 %all-to-all-done.1 = f32[128,17,2,128]{3,2,1,0:T(2,128)S(1)} async-done(((f32[128,17,2,128]{3,2,1,0:T(2,128)}), f32[128,17,2,128]{3,2,1,0:T(2,128)S(1)}, u32[]{:S(2)}, u32[]{:S(2)}) %all-to-all-start.1) | async-done | bytes 2228256 | tf_op jit(solution)/shard_map/all_to_all | solution.py:326
  85.6 0.0 copy-done.12
  85.6 4.1 %shard_map.123 = (f32[1024,256]{1,0:T(8,128)}, f32[192,128]{1,0:T(8,128)S(1)}, f32[2,128]{1,0:T(2,128)S(1)}) custom-call(f32[4352,128]{1,0:T(8,128)S(1)} %bitcast.15, s32[8,128]{1,0:T(8,128)S(1)} %bitcast.22, f32[2,128]{1,0:T(2,128)S(1)} %bitcast.29, f32[2,128]{1,0:T(2,128)S(1)} %bitcast.30, f32[1]{0:T(128)} %get-tuple-element.18.mass_ref, f32[1]{0:T(128)S(6)} %copy.13.level_ref), custom_call_target="tpu_custom_call" | custom-call | tf_op jit(solution)/shard_map/pallas_call | solution.py:395
  89.7 9.4 %all_to_all.20 = f32[8,24,128]{2,1,0:T(8,128)S(1)} all-to-all(f32[8,24,128]{2,1,0:T(8,128)S(1)} %bitcast.19), channel_id=1, replica_groups=mesh['scen'=8,'opt'=16] {'scen'}, dimensions={0} | all-to-all | bytes 196608 | tf_op jit(solution)/shard_map/all_to_all | solution.py:326
  99.1 1.2 %copy-done.2 = f32[1024,256]{1,0:T(8,128)S(1)} copy-done((f32[1024,256]{1,0:T(8,128)S(1)}, f32[1024,256]{1,0:T(8,128)}, u32[]{:S(2)}) %copy-start.2) | copy-done | bytes 1048600
  100.3 1.7 %shard_map.124 = (f32[8,128]{1,0:T(8,128)}, f32[32,128]{1,0:T(8,128)S(1)}, f32[1]{0:T(128)}, f32[1]{0:T(128)}) custom-call(f32[192,128]{1,0:T(8,128)S(1)} %bitcast.18, f32[1024,256]{1,0:T(8,128)S(1)} %copy-done.2, f32[8,128]{1,0:T(8,128)S(1)} %bitcast.24, f32[8,128]{1,0:T(8,128)S(1)} %bitcast.26, f32[1]{0:T(128)} %get-tuple-element.18.mass_ref, ...), custom_call_target="tpu_custom_call" | custom-call | tf_op jit(solution)/shard_map/pallas_call | solution.py:408
  102.0 12.0 %all_to_all.21 = f32[16,2,128]{2,1,0:T(2,128)S(1)} all-to-all(f32[16,2,128]{2,1,0:T(2,128)S(1)} %bitcast.27), channel_id=1, replica_groups=mesh['scen'=8,'opt'=16] {'opt'}, dimensions={0} | all-to-all | bytes 32768 | tf_op jit(solution)/shard_map/all_to_all | solution.py:326
  114.0 1.2 %shard_map.125 = f32[2,128]{1,0:T(2,128)} custom-call(f32[32,128]{1,0:T(8,128)S(1)} %bitcast.20, f32[2,128]{1,0:T(2,128)S(1)} %get-tuple-element.23.dual_ref, f32[2,128]{1,0:T(2,128)S(1)} %bitcast.31, f32[1]{0:T(128)} %get-tuple-element.24.bar_ref), custom_call_target="tpu_custom_call" | custom-call | tf_op jit(solution)/shard_map/pallas_call | solution.py:417
  (18 shorter events, 0.0 us)
Async XLA Ops:
  0.6 1.0 copy-start.3
  1.7 0.7 copy-start.4
  2.4 0.7 copy-start.6
  3.0 0.7 copy-start.8
  3.7 0.7 copy-start.10
  4.4 13.4 %copy-start.13 = (f32[1,2048]{1,0:T(1,128)S(1)}, f32[1,2048]{1,0:T(1,128)}, u32[]{:S(2)}) copy-start(f32[1,2048]{1,0:T(1,128)} %mean_ref.1) | copy-start | bytes 24580
  4.4 13.4 %copy-start.14 = (f32[1,2048]{1,0:T(1,128)S(1)}, f32[1,2048]{1,0:T(1,128)}, u32[]{:S(2)}) copy-start(f32[1,2048]{1,0:T(1,128)} %spread_ref.1) | copy-start | bytes 24580
  6.3 32.6 %all-to-all-start = ((f32[128,10,2,128]{3,2,1,0:T(2,128)}), f32[128,10,2,128]{3,2,1,0:T(2,128)S(1)}, u32[]{:S(2)}, u32[]{:S(2)}) async-start(f32[128,10,2,128]{3,2,1,0:T(2,128)} %bitcast.4), calls=%async_computation | async-start | bytes 2621440 | tf_op jit(solution)/shard_map/all_to_all | solution.py:326
  24.0 2.0 %copy-start = (bf16[1024,2048]{1,0:T(8,128)(2,1)}, bf16[1024,2048]{1,0:T(8,128)(2,1)S(1)}, u32[]{:S(2)}) copy-start(bf16[1024,2048]{1,0:T(8,128)(2,1)S(1)} %get-tuple-element.15.hi_ref) | copy-start | bytes 12582916
  48.3 1.4 %copy-start.1 = (f32[4352,128]{1,0:T(8,128)}, f32[4352,128]{1,0:T(8,128)S(1)}, u32[]{:S(2)}) copy-start(f32[4352,128]{1,0:T(8,128)S(1)} %get-tuple-element.17) | copy-start | bytes 6684676
  49.7 35.9 %copy-start.5 = (s32[1024,1]{0,1:T(1,128)S(1)}, s32[1024,1]{0,1:T(1,128)}, u32[]{:S(2)}) copy-start(s32[1024,1]{0,1:T(1,128)} %param.10) | copy-start | bytes 12292
  49.7 35.9 %copy-start.11 = (f32[256]{0:T(256)S(1)}, f32[256]{0:T(256)}, u32[]{:S(2)}) copy-start(f32[256]{0:T(256)} %param.16) | copy-start | bytes 3076
  49.7 35.9 %copy-start.12 = (f32[256]{0:T(256)S(1)}, f32[256]{0:T(256)}, u32[]{:S(2)}) copy-start(f32[256]{0:T(256)} %param.15) | copy-start | bytes 3076
  49.7 35.9 %all-to-all-start.1 = ((f32[128,17,2,128]{3,2,1,0:T(2,128)}), f32[128,17,2,128]{3,2,1,0:T(2,128)S(1)}, u32[]{:S(2)}, u32[]{:S(2)}) async-start(f32[128,17,2,128]{3,2,1,0:T(2,128)} %bitcast.17), calls=%async_computation.1 | async-start | bytes 4456448 | tf_op jit(solution)/shard_map/all_to_all | solution.py:326
  54.7 44.3 %copy-start.7 = (f32[1024]{0:T(1024)S(1)}, f32[1024]{0:T(1024)}, u32[]{:S(2)}) copy-start(f32[1024]{0:T(1024)} %param.13) | copy-start | bytes 12292
  54.7 44.3 %copy-start.9 = (f32[1024]{0:T(1024)S(1)}, f32[1024]{0:T(1024)}, u32[]{:S(2)}) copy-start(f32[1024]{0:T(1024)} %param.14) | copy-start | bytes 12292
  99.1 1.2 %copy-start.2 = (f32[1024,256]{1,0:T(8,128)S(1)}, f32[1024,256]{1,0:T(8,128)}, u32[]{:S(2)}) copy-start(f32[1024,256]{1,0:T(8,128)} %get-tuple-element.11.tile_ref) | copy-start | bytes 3145732

commit v2 on v1

v2 whole, which is shorter than its diff:
```python
import math

import jax
import jax.numpy as jnp
from jax import lax
from jax.experimental import pallas as pl
from jax.experimental.pallas import tpu as pltpu
from jax.sharding import PartitionSpec as P

LOW_END = -4.0
HIGH_END = 4.0
TAIL_LEVEL = 0.9
PRIMAL_STEP = 0.5
THRESH_STEP = 0.05
DUAL_STEP = 0.5

LANES = 128
SCEN = 8
OPT = 16
DEVICES = SCEN * OPT
TERMS = 1024
SCENARIOS = 2048
OPTIONS = 16384
MOST = 2
CHUNKS = TERMS // LANES
BASE = 32
TABLE = 512
BLOCKS = SCENARIOS // TABLE
READY = 2
BASE_ROWS = 4 * BASE + 8
PAIR = MOST * CHUNKS
DUAL = PAIR + 1
MSG1 = PAIR + 2
MSG2 = MOST * 16 + 2
PAYLOAD = 24
PARTS = 4
ORDER = ("opt", "scen")
F32 = jnp.float32
BF16 = jnp.bfloat16
HIGHEST = lax.Precision.HIGHEST
NN = (((1,), (0,)), ((), ()))
NT = (((1,), (1,)), ((), ()))


def params(mib):
    return pltpu.CompilerParams(vmem_limit_bytes=int(mib * 1024 * 1024))


def iota(shape, axis):
    return lax.broadcasted_iota(jnp.int32, shape, axis)


def owner_of(place):
    return (place & (SCEN - 1)) * OPT + (place >> 3)


def mm(a, b, dims=NN):
    return lax.dot_general(a, b, dims, preferred_element_type=F32)


def three(x):
    hi = x.astype(BF16)
    rest = x - hi.astype(F32)
    mid = rest.astype(BF16)
    low = (rest - mid.astype(F32)).astype(BF16)
    return hi, mid, low


def pick(onehot, x, dims=NN):
    hi, mid, low = three(x)
    return mm(onehot, hi, dims) + mm(onehot, mid, dims) + mm(onehot, low, dims)


def level_step(level, mass):
    return level - THRESH_STEP * (1.0 - mass / ((1.0 - TAIL_LEVEL) * SCENARIOS))


def primal(position, cost, gradient):
    return jnp.clip(
        position - PRIMAL_STEP * (cost - gradient / math.sqrt(SCENARIOS)), -1.0, 1.0
    )


def dual(weights, base, pnl, level_bar):
    return jnp.clip(
        weights + DUAL_STEP * (base - pnl / math.sqrt(OPTIONS) - level_bar), 0.0, 1.0
    )


def send_kernel(
    own_hbm, coef_hbm, cost_hbm, pos_hbm, dual_hbm, out_hbm,
    own_ref, coef_ref, cost_ref, pos_ref, dual_ref, out_ref, sems, out_sems,
):
    pairs = (
        (own_hbm, own_ref),
        (cost_hbm, cost_ref),
        (pos_hbm, pos_ref),
        (dual_hbm, dual_ref),
        (coef_hbm, coef_ref),
    )
    copies = [pltpu.make_async_copy(a, b, sems.at[i]) for i, (a, b) in enumerate(pairs)]
    for copy in copies:
        copy.start()
    for copy in copies[:4]:
        copy.wait()
    row = lax.axis_index("scen")
    half = lax.axis_index("opt") & 1
    square = (LANES, LANES)
    down, across = iota(square, 0), iota(square, 1)
    same = own_ref[pl.ds(row, 1), :] == owner_of(down)
    before = mm(
        same.astype(F32).astype(BF16), (down < across).astype(F32).astype(BF16)
    )
    cost = jnp.broadcast_to(cost_ref[pl.ds(row, 1), :], square)
    pos = jnp.broadcast_to(pos_ref[pl.ds(row, 1), :], square)
    chosen = [
        jnp.where(same & (before == float(rank)), 1.0, 0.0).astype(BF16)
        for rank in range(MOST)
    ]
    pair = jnp.zeros(square, F32)
    for rank in range(MOST):
        packed = jnp.where(
            down == 2 * rank, cost, jnp.where(down == 2 * rank + 1, pos, 0.0)
        )
        pair = pair + pick(chosen[rank], packed, NT)
    out_ref[pl.ds(PAIR, DEVICES, stride=MSG1), :] = pair
    out_ref[pl.ds(DUAL, DEVICES, stride=MSG1), :] = jnp.broadcast_to(
        dual_ref[pl.ds(half, 1), :], square
    )
    copies[4].wait()
    hi, mid, low = three(coef_ref[...])
    size = DEVICES // PARTS
    outs = []
    for part in range(PARTS):
        for rank in range(MOST):
            some = chosen[rank][part * size : (part + 1) * size, :]
            rows = mm(some, hi) + mm(some, mid) + mm(some, low)
            for chunk in range(CHUNKS):
                start = part * size * MSG1 + rank * CHUNKS + chunk
                out_ref[pl.ds(start, size, stride=MSG1), :] = rows[
                    :, chunk * LANES : (chunk + 1) * LANES
                ]
        at = slice(part * size * MSG1, (part + 1) * size * MSG1)
        outs.append(
            pltpu.make_async_copy(out_ref.at[at], out_hbm.at[at], out_sems.at[part])
        )
        outs[part].start()
    for out in outs:
        out.wait()


def turn(quarters, rest):
    x = rest * (2.0 * math.pi)
    z = x * x
    sin = x * (
        1.0 + z * (-1 / 6 + z * (1 / 120 + z * (-1 / 5040 + z * (1 / 362880))))
    )
    cos = 1.0 + z * (
        -1 / 2 + z * (1 / 24 + z * (-1 / 720 + z * (1 / 40320 - z * (1 / 3628800))))
    )
    swap = (quarters & 1) == 1
    cos_out = jnp.where(swap, sin, cos)
    sin_out = jnp.where(swap, cos, sin)
    cos_out = jnp.where(((quarters + 1) & 2) == 2, -cos_out, cos_out)
    sin_out = jnp.where((quarters & 2) == 2, -sin_out, sin_out)
    return cos_out, sin_out


def base_kernel(mean_ref, spread_ref, out_ref, hi_ref, low_ref):
    shape = (BASE, TABLE)
    mean = mean_ref[...]
    coarse = jnp.round(mean * 2048.0) * (1.0 / 2048.0)
    fine = mean - coarse
    step = iota(shape, 0)
    stepf = step.astype(F32)

    def base(scale, extra):
        turns = (stepf * scale) * coarse
        quarters = jnp.round(turns * 4.0)
        rest = (turns - quarters * 0.25) + (stepf * scale) * fine
        return turn(quarters.astype(jnp.int32) + extra, rest)

    cos_b, sin_b = base(1.0 / 16.0, step)
    cos_a, sin_a = base(BASE / 16.0, jnp.zeros_like(step))
    unit = math.pi / (HIGH_END - LOW_END)
    rate = spread_ref[...] * (-0.5 * unit * unit * math.log2(math.e))
    out_ref[0, 0:BASE, :] = cos_a * 0.25
    out_ref[0, BASE : 2 * BASE, :] = sin_a * 0.25
    out_ref[0, 2 * BASE : 3 * BASE, :] = cos_b
    out_ref[0, 3 * BASE : 4 * BASE, :] = sin_b
    out_ref[0, 4 * BASE :, :] = jnp.broadcast_to(rate, (8, TABLE))

    @pl.when(pl.program_id(0) < READY)
    def _():
        table(out_ref.at[0], hi_ref.at[0], low_ref.at[0])


def choice_kernel(own_ref, out_ref):
    square = (LANES, LANES)
    down, across = iota(square, 0), iota(square, 1)
    names = jnp.concatenate(
        [own_ref[...].astype(F32), jnp.zeros((LANES - SCEN, LANES), F32)], axis=0
    ).T
    lower = (across < down).astype(F32).astype(BF16)
    owner = across.astype(F32)
    for s in range(SCEN):
        same = names[:, s : s + 1] == owner
        before = mm(lower, same.astype(F32).astype(BF16))
        for rank in range(MOST):
            out_ref[s, :, rank * LANES : (rank + 1) * LANES] = jnp.where(
                same & (before == float(rank)), 1.0, 0.0
            ).astype(BF16)


def table(base_ref, hi_ref, low_ref):
    step = iota((BASE, LANES), 0)
    stepf = step.astype(F32)
    for half in range(TABLE // LANES):
        at = slice(half * LANES, (half + 1) * LANES)
        cos_b = base_ref[2 * BASE : 3 * BASE, at]
        sin_b = base_ref[3 * BASE : 4 * BASE, at]
        rate = base_ref[4 * BASE : 4 * BASE + 1, at]
        for a in range(BASE):
            k = stepf + float(BASE * a)
            value = (
                base_ref[a : a + 1, at] * cos_b
                - base_ref[BASE + a : BASE + a + 1, at] * sin_b
            ) * jnp.exp2((k * k) * rate)
            if a == 0:
                value = jnp.where(step == 0, value * 0.5, value)
            hi = value.astype(BF16)
            hi_ref[a * BASE : (a + 1) * BASE, at] = hi
            low_ref[a * BASE : (a + 1) * BASE, at] = (value - hi.astype(F32)).astype(BF16)


def value_kernel(
    in_hbm, base_hbm, hi_hbm, low_hbm, out_hbm, mass_ref,
    in_ref, base_ref, hi_0, low_0, hi_1, low_1, hi_made, low_made, coef, values, grad, out_ref, sems, out_sems,
):
    width = 2 * LANES
    rows = MOST * LANES
    firsts = [
        pltpu.make_async_copy(base_hbm.at[READY], base_ref.at[0], sems.at[2, 0]),
        pltpu.make_async_copy(in_hbm, in_ref, sems.at[2, 1]),
        pltpu.make_async_copy(base_hbm.at[READY + 1], base_ref.at[1], sems.at[3, 0]),
    ]
    for copy in firsts:
        copy.start()
    copies = [
        (
            pltpu.make_async_copy(hi_hbm.at[block], hi_made.at[block], sems.at[0, block]),
            pltpu.make_async_copy(low_hbm.at[block], low_made.at[block], sems.at[1, block]),
        )
        for block in range(READY)
    ]
    for pair in copies:
        for copy in pair:
            copy.start()
    firsts[0].wait()
    table(base_ref.at[0], hi_0, low_0)
    firsts[1].wait()
    for rank in range(MOST):
        for chunk in range(CHUNKS):
            part = in_ref[pl.ds(rank * CHUNKS + chunk, DEVICES, stride=MSG1), :]
            hi = part.astype(BF16)
            at = slice(chunk * LANES, (chunk + 1) * LANES)
            coef[rank * LANES : (rank + 1) * LANES, at] = hi
            coef[rows + rank * LANES : rows + (rank + 1) * LANES, at] = (
                part - hi.astype(F32)
            ).astype(BF16)
    grad[...] = jnp.zeros_like(grad)
    firsts[2].wait()

    def multiply(block, hi_ref, low_ref):
        both = mm(coef[...], hi_ref[...])
        wide = both[:rows] + both[rows:] + mm(coef[:rows, :], low_ref[...])
        total = grad[...]
        for part in range(TABLE // width):
            s = block * (TABLE // width) + part
            tile = wide[:, part * width : (part + 1) * width]
            values[s] = tile
            for half in range(2):
                weights = in_ref[pl.ds((half * SCEN + s) * MSG1 + DUAL, 1), :]
                total = total + tile[:, half * LANES : (half + 1) * LANES] * weights
            start = s * OPT * MSG2
            for o in range(OPT):
                for rank in range(MOST):
                    for half in range(2):
                        out_ref[
                            pl.ds(start + o * MSG2 + (rank * 2 + half) * 8, 8), :
                        ] = tile[
                            rank * LANES + o * 8 : rank * LANES + o * 8 + 8,
                            half * LANES : (half + 1) * LANES,
                        ]
        grad[...] = total

    tiles = out_ref.reshape(DEVICES // 4, 17, 8, LANES)
    outs = []

    def send(*view):
        outs.append(
            pltpu.make_async_copy(tiles.at[view], out_hbm.at[view], out_sems.at[len(outs)])
        )
        outs[-1].start()

    def send_values(block):
        share = DEVICES // 4 // BLOCKS
        for first, last in ((0, 4), (5, 8), (9, 12), (13, 16)):
            send(slice(block * share, (block + 1) * share), slice(first, last))

    multiply(READY, hi_0, low_0)
    send_values(READY)
    table(base_ref.at[1], hi_1, low_1)
    multiply(READY + 1, hi_1, low_1)
    send_values(READY + 1)
    for block in range(READY):
        for copy in copies[block]:
            copy.wait()
        multiply(block, hi_made.at[block], low_made.at[block])
        send_values(block)

    mass = jnp.zeros((1, LANES), F32)
    for place in range(2 * SCEN):
        at = place * MSG1 + DUAL
        mass = mass + in_ref[at : at + 1, :]
    mass_ref[0] = jnp.sum(mass)
    extra = in_ref[pl.ds(PAIR, DEVICES, stride=MSG1), :]
    bars = []
    for rank in range(MOST):
        cost, pos = extra[:, 2 * rank : 2 * rank + 1], extra[:, 2 * rank + 1 : 2 * rank + 2]
        gradient = jnp.sum(
            grad[rank * LANES : (rank + 1) * LANES, :], axis=1, keepdims=True
        )
        bars.append(2.0 * primal(pos, cost, gradient) - pos)
    bar = jnp.broadcast_to(jnp.concatenate(bars, axis=0), (rows, LANES))
    for s in range(SCEN):
        for half in range(2):
            pnl = values[s, :, half * LANES : (half + 1) * LANES] * bar
            out_ref[pl.ds(s * OPT * MSG2 + MSG2 - 2 + half, OPT, stride=MSG2), :] = (
                jnp.broadcast_to(jnp.sum(pnl, axis=0, keepdims=True), (OPT, LANES))
            )
    for tile in (4, 8, 12, 16):
        send(slice(0, DEVICES // 4), slice(tile, tile + 1))
    for out in outs:
        out.wait()


def tile_kernel(
    in_ref, choice_ref, dual_ref, base_ref, mass_ref, level_ref, tile_ref, pay_ref, dual_out
):
    level = level_ref[0]
    level_bar = 2.0 * level_step(level, mass_ref[0]) - level
    weights = []
    for half in range(2):
        pnl = jnp.sum(
            in_ref[pl.ds(MSG2 - 2 + half, DEVICES, stride=MSG2), :], axis=0, keepdims=True
        )
        weights.append(
            dual(dual_ref[half : half + 1, :], base_ref[half : half + 1, :], pnl, level_bar)
        )
        dual_out[half : half + 1, :] = weights[half]
    new = jnp.concatenate(weights, axis=1)
    old = jnp.concatenate([dual_ref[0:1, :], dual_ref[1:2, :]], axis=1)
    tall = iota((8, 2 * LANES), 0)
    both = jnp.where(
        tall == 0,
        jnp.broadcast_to(old, (8, 2 * LANES)),
        jnp.where(tall == 1, jnp.broadcast_to(new, (8, 2 * LANES)), 0.0),
    )
    rows = []
    for s in range(SCEN):
        arrived = jnp.concatenate(
            [
                jnp.concatenate(
                    [
                        in_ref[pl.ds((rank * 2 + half) * 8 + s, DEVICES, stride=MSG2), :]
                        for half in range(2)
                    ],
                    axis=1,
                )
                for rank in range(MOST)
            ],
            axis=0,
        )
        tile = pick(choice_ref[s], arrived)
        tile_ref[s * LANES : (s + 1) * LANES, :] = tile
        rows.append(
            lax.dot_general(both, tile, NT, precision=HIGHEST, preferred_element_type=F32)
        )
    payload = jnp.concatenate(
        [r[0:1, :] for r in rows]
        + [r[1:2, :] for r in rows]
        + [weights[0] + weights[1], jnp.zeros((PAYLOAD - 17, LANES), F32)],
        axis=0,
    )
    for s in range(SCEN):
        pay_ref[s * PAYLOAD : (s + 1) * PAYLOAD, :] = payload


def position_kernel(
    in_ref, tile_ref, cost_ref, pos_ref, mass_ref, level_ref,
    pos_out, pnl_out, tile_hbm, level_out, bar_out, sem,
):
    keep = pltpu.make_async_copy(tile_ref, tile_hbm, sem)
    keep.start()
    total = in_ref[0:PAYLOAD, :]
    for s in range(1, SCEN):
        total = total + in_ref[s * PAYLOAD : (s + 1) * PAYLOAD, :]
    level = level_step(level_ref[0], mass_ref[0])
    later = level_step(level, jnp.sum(total[16:17, :]))
    level_out[0] = later
    bar_out[0] = 2.0 * later - level
    cost = cost_ref[...]
    first = primal(pos_ref[...], cost, total[0:8, :])
    second = primal(first, cost, total[8:16, :])
    pos_out[...] = second
    bar = 2.0 * second - first
    pnl = jnp.zeros((1, 2 * LANES), F32)
    for s in range(SCEN):
        pnl = pnl + lax.dot_general(
            bar[s : s + 1, :],
            tile_ref[s * LANES : (s + 1) * LANES, :],
            NN,
            precision=HIGHEST,
            preferred_element_type=F32,
        )
    for o in range(OPT):
        for half in range(2):
            pnl_out[o * 2 + half : o * 2 + half + 1, :] = pnl[:, half * LANES : (half + 1) * LANES]
    keep.wait()


def dual_kernel(in_ref, dual_ref, base_ref, bar_ref, out_ref):
    pnl = in_ref[0:2, :]
    for o in range(1, OPT):
        pnl = pnl + in_ref[2 * o : 2 * o + 2, :]
    out_ref[...] = dual(dual_ref[...], base_ref[...], pnl, bar_ref[0])


VMEM = pl.BlockSpec(memory_space=pltpu.VMEM)
HBM = pl.BlockSpec(memory_space=pltpu.HBM)
SMEM = pl.BlockSpec(memory_space=pltpu.SMEM)


def exchange(x, axes):
    return lax.all_to_all(x, axes, split_axis=0, concat_axis=0, tiled=True)


def shaped(*shape, dtype=F32):
    return jax.ShapeDtypeStruct(shape, dtype)


def value_scratch():
    return [
        pltpu.VMEM((DEVICES * MSG1, LANES), F32),
        pltpu.VMEM((BLOCKS - READY, BASE_ROWS, TABLE), F32),
        *[pltpu.VMEM((TERMS, TABLE), BF16)] * 4,
        *[pltpu.VMEM((READY, TERMS, TABLE), BF16)] * 2,
        pltpu.VMEM((2 * MOST * LANES, TERMS), BF16),
        pltpu.VMEM((SCEN, MOST * LANES, 2 * LANES), F32),
        pltpu.VMEM((MOST * LANES, LANES), F32),
        pltpu.VMEM((DEVICES * MSG2, LANES), F32),
        pltpu.SemaphoreType.DMA((4, 2)),
        pltpu.SemaphoreType.DMA((4 * BLOCKS + 4,)),
    ]


def on_device(
    option_coefs,
    underlying_of,
    log_return_mean,
    log_return_spread,
    cost,
    positions,
    base_loss,
    duals,
    threshold,
):
    own = underlying_of.reshape(SCEN, LANES)
    cost = cost.reshape(SCEN, LANES)
    positions = positions.reshape(SCEN, LANES)
    base_loss = base_loss.reshape(2, LANES)
    duals = duals.reshape(2, LANES)

    sent = pl.pallas_call(
        send_kernel,
        out_shape=shaped(DEVICES * MSG1, LANES),
        in_specs=[HBM] * 5,
        out_specs=HBM,
        scratch_shapes=[
            pltpu.VMEM((SCEN, LANES), jnp.int32),
            pltpu.VMEM((LANES, TERMS), F32),
            pltpu.VMEM((SCEN, LANES), F32),
            pltpu.VMEM((SCEN, LANES), F32),
            pltpu.VMEM((2, LANES), F32),
            pltpu.VMEM((DEVICES * MSG1, LANES), F32),
            pltpu.SemaphoreType.DMA((5,)),
            pltpu.SemaphoreType.DMA((PARTS,)),
        ],
        compiler_params=params(63),
    )(own, option_coefs, cost, positions, duals)
    got = exchange(sent.reshape(DEVICES, MSG1 // 2, 2, LANES), ORDER)
    got = got.reshape(DEVICES * MSG1, LANES)

    made = pl.BlockSpec((1, TERMS, TABLE), lambda i: (jnp.minimum(i, READY - 1), 0, 0))
    base, made_hi, made_low = pl.pallas_call(
        base_kernel,
        grid=(BLOCKS,),
        out_shape=[
            pltpu.HBM((BLOCKS, BASE_ROWS, TABLE), F32),
            *[pltpu.HBM((READY, TERMS, TABLE), BF16)] * 2,
        ],
        in_specs=[pl.BlockSpec((1, TABLE), lambda i: (0, i))] * 2,
        out_specs=[pl.BlockSpec((1, BASE_ROWS, TABLE), lambda i: (i, 0, 0)), made, made],
        compiler_params=params(12),
        cost_estimate=pl.CostEstimate(
            flops=2 * TERMS * SCENARIOS,
            bytes_accessed=TERMS * SCENARIOS,
            transcendentals=0,
        ),
    )(log_return_mean, log_return_spread)
    choice = pl.pallas_call(
        choice_kernel,
        out_shape=shaped(SCEN, LANES, MOST * LANES, dtype=BF16),
        in_specs=[VMEM],
        out_specs=VMEM,
        compiler_params=params(4),
        cost_estimate=pl.CostEstimate(
            flops=TERMS * SCENARIOS, bytes_accessed=SCENARIOS, transcendentals=0
        ),
    )(own)

    values, mass = pl.pallas_call(
        value_kernel,
        out_shape=[shaped(DEVICES // 4, 17, 8, LANES), shaped(1)],
        in_specs=[HBM] * 4,
        out_specs=[HBM, SMEM],
        scratch_shapes=value_scratch(),
        compiler_params=params(63),
    )(got, base, made_hi, made_low)
    arrived = exchange(values.reshape(DEVICES, MSG2 // 2, 2, LANES), ("scen", "opt"))
    arrived = arrived.reshape(DEVICES * MSG2, LANES)

    tile, payload, first_duals = pl.pallas_call(
        tile_kernel,
        out_shape=[
            shaped(SCEN * LANES, 2 * LANES),
            shaped(SCEN * PAYLOAD, LANES),
            shaped(2, LANES),
        ],
        in_specs=[VMEM] * 4 + [SMEM] * 2,
        out_specs=[VMEM] * 3,
        compiler_params=params(12),
    )(arrived, choice, duals, base_loss, mass, threshold)
    gathered = exchange(payload.reshape(SCEN, PAYLOAD, LANES), "scen")

    new_positions, part_pnl, kept, level, level_bar = pl.pallas_call(
        position_kernel,
        out_shape=[
            shaped(SCEN, LANES),
            shaped(OPT * 2, LANES),
            shaped(SCEN * LANES, 2 * LANES),
            shaped(1),
            shaped(1),
        ],
        in_specs=[VMEM] * 4 + [SMEM] * 2,
        out_specs=[VMEM] * 2 + [HBM] + [SMEM] * 2,
        scratch_shapes=[pltpu.SemaphoreType.DMA(())],
        compiler_params=params(8),
    )(gathered.reshape(SCEN * PAYLOAD, LANES), tile, cost, positions, mass, threshold)
    pnl = exchange(part_pnl.reshape(OPT, 2, LANES), "opt")

    new_duals = pl.pallas_call(
        dual_kernel,
        out_shape=shaped(2, LANES),
        in_specs=[VMEM] * 3 + [SMEM],
        out_specs=VMEM,
        compiler_params=params(8),
    )(pnl.reshape(OPT * 2, LANES), first_duals, base_loss, level_bar)
    return (kept, new_positions.reshape(-1), new_duals.reshape(-1), level)


def solution(mesh):
    in_specs = (
        P(("opt", "scen"), None),
        P("opt", None),
        P(("scen", "opt"), None),
        P(("scen", "opt"), None),
        P("opt"),
        P("opt"),
        P("scen"),
        P("scen"),
        P(),
    )
    out_specs = (P("opt", "scen"), P("opt"), P("scen"), P())
    return jax.shard_map(
        on_device, mesh=mesh, in_specs=in_specs, out_specs=out_specs, check_vma=False
    )
```

time: 116 us -> 108 us (0.931)
  local copies, waits for them, and re-layouts: 8.42 us -> 0.04 us
  waiting for transfers between devices: 43.1 us -> 46.5 us
  Pallas kernels: 24.4 us -> 22.2 us
  blocking collectives: 21.3 us -> 19.9 us
    unnamed x30 -> x14, local copies, waits for them, and re-layouts: 8.42 us -> 0.04 us
    pallas_call x3 -> x4, Pallas kernels: 19.6 us -> 15.8 us  [the longest x1 8.14 us: on_device(): pl.pallas_call(value_kernel, out_shape=[shaped(DEVICES // 4, 17, 8, LANES...]
    all_to_all x2, waiting for transfers between devices: 43.1 us -> 46.5 us  [exchange(): return lax.all_to_all(x, axes, split_axis=0, concat_axis=0, tiled=True)]
    all_to_all x2, blocking collectives: 21.3 us -> 19.9 us  [exchange(): return lax.all_to_all(x, axes, split_axis=0, concat_axis=0, tiled=True)]
where the time goes in v2:
time: 108 us; the launch traced here: 107 us
  waiting for transfers between devices  46.5 us (43%)
  Pallas kernels  22.2 us (21%)
  blocking collectives  19.9 us (18%)
  starting transfers between devices  17 us (16%)
  between operations  1.43 us (1%)
    all_to_all x2, waiting for transfers between devices, exchange(): return lax.all_to_all(x, axes, split_axis=0, concat_axis=0, tiled=True)  46.5 us
    all_to_all x2, blocking collectives, exchange(): return lax.all_to_all(x, axes, split_axis=0, concat_axis=0, tiled=True)  19.9 us
    all_to_all x2, starting transfers between devices, exchange(): return lax.all_to_all(x, axes, split_axis=0, concat_axis=0, tiled=True)  17 us
    pallas_call x1, Pallas kernels, on_device(): pl.pallas_call(value_kernel, out_shape=[shaped(DEVICES // 4, 17, 8, LANES...  8.14 us
    pallas_call x1, Pallas kernels, on_device(): pl.pallas_call(base_kernel, grid=(BLOCKS,), out_shape=[pltpu.HBM((BLOCKS,...  4.39 us
    pallas_call x1, Pallas kernels, on_device(): pl.pallas_call(send_kernel, out_shape=shaped(DEVICES * MSG1, LANES), in_s...  2.93 us
    pallas_call x1, Pallas kernels, on_device(): pl.pallas_call(tile_kernel, out_shape=[shaped(SCEN * LANES, 2 * LANES), s...  2.66 us
    pallas_call x1, Pallas kernels, on_device(): pl.pallas_call(position_kernel, out_shape=[shaped(SCEN, LANES), shaped(OP...  2.26 us
  transfers between devices with their start and end apart: 2, of which 2 were waited for; matrix products, arithmetic and copies ran while one was open for 0% of the time, Pallas kernels for 5%

profile of v2, /device:TPU:1, one launch (start us, length us, event | category | flops | bytes accessed | tf_op | source)
XLA Modules:
  0.0 107.2 jit_solution(6208403343334472255)
XLA Ops:
  0.6 0.0 copy-start.3
  0.6 0.0 copy-start.4
  0.7 2.9 %shard_map.120 = f32[2304,128]{1,0:T(8,128)} custom-call(s32[8,128]{1,0:T(8,128)} %bitcast.19, f32[128,1024]{1,0:T(8,128)} %coef_hbm.1, f32[8,128]{1,0:T(8,128)} %bitcast.21, f32[8,128]{1,0:T(8,128)} %bitcast.23, f32[2,128]{1,0:T(2,128)} %bitcast.26), custom_call_target="tpu_custom_call" | custom-call | tf_op jit(solution)/shard_map/pallas_call | solution.py:485
  3.6 11.9 %all-to-all-start = ((f32[128,9,2,128]{3,2,1,0:T(2,128)}), f32[128,9,2,128]{3,2,1,0:T(2,128)}, u32[]{:S(2)}, u32[]{:S(2)}) async-start(f32[128,9,2,128]{3,2,1,0:T(2,128)} %bitcast.30), calls=%async_computation | async-start | bytes 2359296 | tf_op jit(solution)/shard_map/all_to_all | solution.py:446
  15.5 0.0 copy-done.3
  15.5 0.0 copy-done.4
  15.5 4.4 %shard_map.121 = (f32[4,136,512]{2,1,0:T(8,128)}, bf16[2,1024,512]{2,1,0:T(8,128)(2,1)}, bf16[2,1024,512]{2,1,0:T(8,128)(2,1)}) custom-call(f32[1,2048]{1,0:T(1,128)S(1)} %copy-done.3, f32[1,2048]{1,0:T(1,128)S(1)} %copy-done.4), custom_call_target="tpu_custom_call" | custom-call | flops 4194304 | bytes 2097152 | tf_op jit(solution)/shard_map/pallas_call | solution.py:506
  19.9 15.0 %all-to-all-done = f32[128,9,2,128]{3,2,1,0:T(2,128)} async-done(((f32[128,9,2,128]{3,2,1,0:T(2,128)}), f32[128,9,2,128]{3,2,1,0:T(2,128)}, u32[]{:S(2)}, u32[]{:S(2)}) %all-to-all-start) | async-done | bytes 1179680 | tf_op jit(solution)/shard_map/all_to_all | solution.py:446
  34.9 8.1 %shard_map.122 = (f32[32,17,8,128]{3,2,1,0:T(8,128)}, f32[1]{0:T(128)}) custom-call(f32[2304,128]{1,0:T(8,128)} %bitcast.5.in_hbm, f32[4,136,512]{2,1,0:T(8,128)} %get-tuple-element.17.base_hbm, bf16[2,1024,512]{2,1,0:T(8,128)(2,1)} %get-tuple-element.18.hi_hbm, bf16[2,1024,512]{2,1,0:T(8,128)(2,1)} %get-tuple-element.19.low_hbm), custom_call_target="tpu_custom_call" | custom-call | tf_op jit(solution)/shard_map/pallas_call | solution.py:533
  43.0 0.0 copy-start
  43.0 0.0 copy-start.5
  43.0 0.0 copy-start.6
  43.1 5.1 %all-to-all-start.1 = ((f32[128,17,2,128]{3,2,1,0:T(2,128)}), f32[128,17,2,128]{3,2,1,0:T(2,128)S(1)}, u32[]{:S(2)}, u32[]{:S(2)}) async-start(f32[128,17,2,128]{3,2,1,0:T(2,128)} %bitcast.31), calls=%async_computation.1 | async-start | bytes 4456448 | tf_op jit(solution)/shard_map/all_to_all | solution.py:446
  48.2 0.0 copy-start.1
  48.2 0.0 copy-start.2
  48.9 0.0 copy-done
  48.9 0.6 shard_map.123.choice_ref
  49.5 31.6 %all-to-all-done.1 = f32[128,17,2,128]{3,2,1,0:T(2,128)S(1)} async-done(((f32[128,17,2,128]{3,2,1,0:T(2,128)}), f32[128,17,2,128]{3,2,1,0:T(2,128)S(1)}, u32[]{:S(2)}, u32[]{:S(2)}) %all-to-all-start.1) | async-done | bytes 2228256 | tf_op jit(solution)/shard_map/all_to_all | solution.py:446
  81.1 0.0 copy-done.6
  81.1 2.7 %shard_map.124 = (f32[1024,256]{1,0:T(8,128)S(1)}, f32[192,128]{1,0:T(8,128)S(1)}, f32[2,128]{1,0:T(2,128)S(1)}) custom-call(f32[4352,128]{1,0:T(8,128)S(1)} %bitcast.15, bf16[8,128,256]{2,1,0:T(8,128)(2,1)S(1)} %shard_map.123.choice_ref, f32[2,128]{1,0:T(2,128)S(1)} %bitcast.27, f32[2,128]{1,0:T(2,128)S(1)} %bitcast.28, f32[1]{0:T(128)} %get-tuple-element.21.mass_ref, ...), custom_call_target="tpu_custom_call" | custom-call | tf_op jit(solution)/shard_map/pallas_call | solution.py:544
  83.7 7.7 %all_to_all.20 = f32[8,24,128]{2,1,0:T(8,128)S(1)} all-to-all(f32[8,24,128]{2,1,0:T(8,128)S(1)} %bitcast.17), channel_id=1, replica_groups=mesh['scen'=8,'opt'=16] {'scen'}, dimensions={0} | all-to-all | bytes 196608 | tf_op jit(solution)/shard_map/all_to_all | solution.py:446
  91.4 2.3 %shard_map.125 = (f32[8,128]{1,0:T(8,128)}, f32[32,128]{1,0:T(8,128)S(1)}, f32[1024,256]{1,0:T(8,128)}, f32[1]{0:T(128)}, f32[1]{0:T(128)}) custom-call(f32[192,128]{1,0:T(8,128)S(1)} %bitcast.16, f32[1024,256]{1,0:T(8,128)S(1)} %get-tuple-element.23.tile_ref, f32[8,128]{1,0:T(8,128)S(1)} %bitcast.22, f32[8,128]{1,0:T(8,128)S(1)} %bitcast.24, ...), custom_call_target="tpu_custom_call" | custom-call | tf_op jit(solution)/shard_map/pallas_call | solution.py:557
  93.7 12.3 %all_to_all.21 = f32[16,2,128]{2,1,0:T(2,128)S(1)} all-to-all(f32[16,2,128]{2,1,0:T(2,128)S(1)} %bitcast.25), channel_id=1, replica_groups=mesh['scen'=8,'opt'=16] {'opt'}, dimensions={0} | all-to-all | bytes 32768 | tf_op jit(solution)/shard_map/all_to_all | solution.py:446
  106.0 1.2 %shard_map.126 = f32[2,128]{1,0:T(2,128)} custom-call(f32[32,128]{1,0:T(8,128)S(1)} %bitcast.18, f32[2,128]{1,0:T(2,128)S(1)} %get-tuple-element.27.dual_ref, f32[2,128]{1,0:T(2,128)S(1)} %bitcast.29, f32[1]{0:T(128)} %get-tuple-element.28.bar_ref), custom_call_target="tpu_custom_call" | custom-call | tf_op jit(solution)/shard_map/pallas_call | solution.py:573
  (3 shorter events, 0.0 us)
Async XLA Ops:
  0.6 14.9 %copy-start.3 = (f32[1,2048]{1,0:T(1,128)S(1)}, f32[1,2048]{1,0:T(1,128)}, u32[]{:S(2)}) copy-start(f32[1,2048]{1,0:T(1,128)} %mean_ref.1) | copy-start | bytes 24580
  0.6 14.9 %copy-start.4 = (f32[1,2048]{1,0:T(1,128)S(1)}, f32[1,2048]{1,0:T(1,128)}, u32[]{:S(2)}) copy-start(f32[1,2048]{1,0:T(1,128)} %spread_ref.1) | copy-start | bytes 24580
  3.6 31.3 %all-to-all-start = ((f32[128,9,2,128]{3,2,1,0:T(2,128)}), f32[128,9,2,128]{3,2,1,0:T(2,128)}, u32[]{:S(2)}, u32[]{:S(2)}) async-start(f32[128,9,2,128]{3,2,1,0:T(2,128)} %bitcast.30), calls=%async_computation | async-start | bytes 2359296 | tf_op jit(solution)/shard_map/all_to_all | solution.py:446
  43.0 5.9 %copy-start = (s32[1024,1]{0,1:T(1,128)S(1)}, s32[1024,1]{0,1:T(1,128)}, u32[]{:S(2)}) copy-start(s32[1024,1]{0,1:T(1,128)} %param.10) | copy-start | bytes 12292
  43.0 38.0 %copy-start.5 = (f32[256]{0:T(256)S(1)}, f32[256]{0:T(256)}, u32[]{:S(2)}) copy-start(f32[256]{0:T(256)} %param.16) | copy-start | bytes 3076
  43.0 38.0 %copy-start.6 = (f32[256]{0:T(256)S(1)}, f32[256]{0:T(256)}, u32[]{:S(2)}) copy-start(f32[256]{0:T(256)} %param.15) | copy-start | bytes 3076
  43.1 38.0 %all-to-all-start.1 = ((f32[128,17,2,128]{3,2,1,0:T(2,128)}), f32[128,17,2,128]{3,2,1,0:T(2,128)S(1)}, u32[]{:S(2)}, u32[]{:S(2)}) async-start(f32[128,17,2,128]{3,2,1,0:T(2,128)} %bitcast.31), calls=%async_computation.1 | async-start | bytes 4456448 | tf_op jit(solution)/shard_map/all_to_all | solution.py:446
  48.2 43.2 %copy-start.1 = (f32[1024]{0:T(1024)S(1)}, f32[1024]{0:T(1024)}, u32[]{:S(2)}) copy-start(f32[1024]{0:T(1024)} %param.13) | copy-start | bytes 12292
  48.2 43.2 %copy-start.2 = (f32[1024]{0:T(1024)S(1)}, f32[1024]{0:T(1024)}, u32[]{:S(2)}) copy-start(f32[1024]{0:T(1024)} %param.14) | copy-start | bytes 12292

commit v3 on v2

--- a/solution.py
+++ b/solution.py
@@ -34,7 +34,10 @@
 MSG2 = MOST * 16 + 2
 PAYLOAD = 24
 PARTS = 4
-ORDER = ("opt", "scen")
+STORED = 5
+AXES = ("z_lo", "x", "z_hi", "y", "core")
+SIZES = (2, 4, 2, 4, 2)
+SCEN_AXES, OPT_AXES = AXES[:2], AXES[2:]
 F32 = jnp.float32
 BF16 = jnp.bfloat16
 HIGHEST = lax.Precision.HIGHEST
@@ -64,6 +67,11 @@
     mid = rest.astype(BF16)
     low = (rest - mid.astype(F32)).astype(BF16)
     return hi, mid, low
+
+
+def two(x):
+    hi = x.astype(BF16)
+    return hi, (x - hi.astype(F32)).astype(BF16)
 
 
 def pick(onehot, x, dims=NN):
@@ -103,8 +111,8 @@
         copy.start()
     for copy in copies[:4]:
         copy.wait()
-    row = lax.axis_index("scen")
-    half = lax.axis_index("opt") & 1
+    row = lax.axis_index("z_lo") * 4 + lax.axis_index("x")
+    half = lax.axis_index("core")
     square = (LANES, LANES)
     down, across = iota(square, 0), iota(square, 1)
     same = own_ref[pl.ds(row, 1), :] == owner_of(down)
@@ -128,13 +136,13 @@
         dual_ref[pl.ds(half, 1), :], square
     )
     copies[4].wait()
-    hi, mid, low = three(coef_ref[...])
+    hi, mid = two(coef_ref[...])
     size = DEVICES // PARTS
     outs = []
     for part in range(PARTS):
         for rank in range(MOST):
             some = chosen[rank][part * size : (part + 1) * size, :]
-            rows = mm(some, hi) + mm(some, mid) + mm(some, low)
+            rows = mm(some, hi) + mm(some, mid)
             for chunk in range(CHUNKS):
                 start = part * size * MSG1 + rank * CHUNKS + chunk
                 out_ref[pl.ds(start, size, stride=MSG1), :] = rows[
@@ -346,7 +354,8 @@
 
 
 def tile_kernel(
-    in_ref, choice_ref, dual_ref, base_ref, mass_ref, level_ref, tile_ref, pay_ref, dual_out
+    in_ref, choice_ref, dual_ref, base_ref, mass_ref, level_ref,
+    tile_ref, pay_ref, dual_out, tile_hbm, sems,
 ):
     level = level_ref[0]
     level_bar = 2.0 * level_step(level, mass_ref[0]) - level
@@ -367,7 +376,7 @@
         jnp.broadcast_to(old, (8, 2 * LANES)),
         jnp.where(tall == 1, jnp.broadcast_to(new, (8, 2 * LANES)), 0.0),
     )
-    rows = []
+    rows, copies = [], []
     for s in range(SCEN):
         arrived = jnp.concatenate(
             [
@@ -383,7 +392,11 @@
             axis=0,
         )
         tile = pick(choice_ref[s], arrived)
-        tile_ref[s * LANES : (s + 1) * LANES, :] = tile
+        at = slice(s * LANES, (s + 1) * LANES)
+        tile_ref[at, :] = tile
+        if s < STORED:
+            copies.append(pltpu.make_async_copy(tile_ref.at[at], tile_hbm.at[at], sems.at[s]))
+            copies[s].start()
         rows.append(
             lax.dot_general(both, tile, NT, precision=HIGHEST, preferred_element_type=F32)
         )
@@ -395,13 +408,16 @@
     )
     for s in range(SCEN):
         pay_ref[s * PAYLOAD : (s + 1) * PAYLOAD, :] = payload
+    for copy in copies:
+        copy.wait()
 
 
 def position_kernel(
-    in_ref, tile_ref, cost_ref, pos_ref, mass_ref, level_ref,
+    in_ref, tile_ref, cost_ref, pos_ref, kept_ref, mass_ref, level_ref,
     pos_out, pnl_out, tile_hbm, level_out, bar_out, sem,
 ):
-    keep = pltpu.make_async_copy(tile_ref, tile_hbm, sem)
+    rest = slice(STORED * LANES, SCEN * LANES)
+    keep = pltpu.make_async_copy(tile_ref.at[rest], tile_hbm.at[rest], sem)
     keep.start()
     total = in_ref[0:PAYLOAD, :]
     for s in range(1, SCEN):
@@ -415,26 +431,19 @@
     second = primal(first, cost, total[8:16, :])
     pos_out[...] = second
     bar = 2.0 * second - first
-    pnl = jnp.zeros((1, 2 * LANES), F32)
+    pnl = jnp.zeros((8, 2 * LANES), F32)
+    odd = (iota((8, LANES), 0) & 1) == 1
     for s in range(SCEN):
-        pnl = pnl + lax.dot_general(
-            bar[s : s + 1, :],
-            tile_ref[s * LANES : (s + 1) * LANES, :],
-            NN,
-            precision=HIGHEST,
-            preferred_element_type=F32,
-        )
+        line = jnp.broadcast_to(bar[s : s + 1, :], (8, LANES))
+        upper = line.astype(BF16).astype(F32)
+        parts = jnp.where(odd, line - upper, upper).astype(BF16)
+        hi, low = two(tile_ref[s * LANES : (s + 1) * LANES, :])
+        pnl = pnl + mm(parts, hi) + mm(parts, low)
+    pnl = pnl[0:1, :] + pnl[1:2, :]
     for o in range(OPT):
         for half in range(2):
             pnl_out[o * 2 + half : o * 2 + half + 1, :] = pnl[:, half * LANES : (half + 1) * LANES]
     keep.wait()
-
-
-def dual_kernel(in_ref, dual_ref, base_ref, bar_ref, out_ref):
-    pnl = in_ref[0:2, :]
-    for o in range(1, OPT):
-        pnl = pnl + in_ref[2 * o : 2 * o + 2, :]
-    out_ref[...] = dual(dual_ref[...], base_ref[...], pnl, bar_ref[0])
 
 
 VMEM = pl.BlockSpec(memory_space=pltpu.VMEM)
@@ -499,7 +508,7 @@
         ],
         compiler_params=params(63),
     )(own, option_coefs, cost, positions, duals)
-    got = exchange(sent.reshape(DEVICES, MSG1 // 2, 2, LANES), ORDER)
+    got = exchange(sent.reshape(DEVICES, MSG1 // 2, 2, LANES), OPT_AXES + SCEN_AXES)
     got = got.reshape(DEVICES * MSG1, LANES)
 
     made = pl.BlockSpec((1, TERMS, TABLE), lambda i: (jnp.minimum(i, READY - 1), 0, 0))
@@ -538,21 +547,23 @@
         scratch_shapes=value_scratch(),
         compiler_params=params(63),
     )(got, base, made_hi, made_low)
-    arrived = exchange(values.reshape(DEVICES, MSG2 // 2, 2, LANES), ("scen", "opt"))
+    arrived = exchange(values.reshape(DEVICES, MSG2 // 2, 2, LANES), AXES)
     arrived = arrived.reshape(DEVICES * MSG2, LANES)
 
-    tile, payload, first_duals = pl.pallas_call(
+    tile, payload, first_duals, kept = pl.pallas_call(
         tile_kernel,
         out_shape=[
             shaped(SCEN * LANES, 2 * LANES),
             shaped(SCEN * PAYLOAD, LANES),
             shaped(2, LANES),
+            shaped(SCEN * LANES, 2 * LANES),
         ],
         in_specs=[VMEM] * 4 + [SMEM] * 2,
-        out_specs=[VMEM] * 3,
+        out_specs=[VMEM] * 3 + [HBM],
+        scratch_shapes=[pltpu.SemaphoreType.DMA((STORED,))],
         compiler_params=params(12),
     )(arrived, choice, duals, base_loss, mass, threshold)
-    gathered = exchange(payload.reshape(SCEN, PAYLOAD, LANES), "scen")
+    gathered = exchange(payload.reshape(SCEN, PAYLOAD, LANES), SCEN_AXES[::-1])
 
     new_positions, part_pnl, kept, level, level_bar = pl.pallas_call(
         position_kernel,
@@ -563,36 +574,33 @@
             shaped(1),
             shaped(1),
         ],
-        in_specs=[VMEM] * 4 + [SMEM] * 2,
+        in_specs=[VMEM] * 4 + [HBM] + [SMEM] * 2,
         out_specs=[VMEM] * 2 + [HBM] + [SMEM] * 2,
+        input_output_aliases={4: 2},
         scratch_shapes=[pltpu.SemaphoreType.DMA(())],
         compiler_params=params(8),
-    )(gathered.reshape(SCEN * PAYLOAD, LANES), tile, cost, positions, mass, threshold)
-    pnl = exchange(part_pnl.reshape(OPT, 2, LANES), "opt")
-
-    new_duals = pl.pallas_call(
-        dual_kernel,
-        out_shape=shaped(2, LANES),
-        in_specs=[VMEM] * 3 + [SMEM],
-        out_specs=VMEM,
-        compiler_params=params(8),
-    )(pnl.reshape(OPT * 2, LANES), first_duals, base_loss, level_bar)
+    )(gathered.reshape(SCEN * PAYLOAD, LANES), tile, cost, positions, kept, mass, threshold)
+    pnl = exchange(part_pnl.reshape(OPT, 2, LANES), OPT_AXES[::-1])
+
+    new_duals = dual(first_duals, base_loss, jnp.sum(pnl, axis=0), level_bar)
     return (kept, new_positions.reshape(-1), new_duals.reshape(-1), level)
 
 
 def solution(mesh):
+    mesh = jax.sharding.Mesh(mesh.devices.reshape(SIZES), AXES)
+    scen, opt = SCEN_AXES, OPT_AXES
     in_specs = (
-        P(("opt", "scen"), None),
-        P("opt", None),
-        P(("scen", "opt"), None),
-        P(("scen", "opt"), None),
-        P("opt"),
-        P("opt"),
-        P("scen"),
-        P("scen"),
+        P(opt + scen, None),
+        P(opt, None),
+        P(AXES, None),
+        P(AXES, None),
+        P(opt),
+        P(opt),
+        P(scen),
+        P(scen),
         P(),
     )
-    out_specs = (P("opt", "scen"), P("opt"), P("scen"), P())
+    out_specs = (P(opt, scen), P(opt), P(scen), P())
     return jax.shard_map(
         on_device, mesh=mesh, in_specs=in_specs, out_specs=out_specs, check_vma=False
     )

time: 108 us -> 107 us (level)
  Pallas kernels: 22.2 us -> 20.7 us
  other arithmetic: 0 us -> 1.23 us
    pallas_call x1 -> x0, Pallas kernels: 1.21 us -> none  [on_device(): pl.pallas_call(dual_kernel, out_shape=shaped(2, LANES), in_specs=[VMEM] *...]
    reshape x0 -> x1, other arithmetic: none -> 1.2 us  [on_device(): return (kept, new_positions.reshape(-1), new_duals.reshape(-1), level)]
where the time goes in v3:
time: 107 us
  waiting for transfers between devices  46.5 us (43%)
  Pallas kernels  20.7 us (19%)
  blocking collectives  19.6 us (18%)
  starting transfers between devices  17 us (16%)
  between operations  1.43 us (1%)
  other arithmetic  1.23 us (1%)
    all_to_all x2, waiting for transfers between devices, exchange(): return lax.all_to_all(x, axes, split_axis=0, concat_axis=0, tiled=True)  46.5 us
    all_to_all x2, blocking collectives, exchange(): return lax.all_to_all(x, axes, split_axis=0, concat_axis=0, tiled=True)  19.6 us
    all_to_all x2, starting transfers between devices, exchange(): return lax.all_to_all(x, axes, split_axis=0, concat_axis=0, tiled=True)  17 us
    pallas_call x1, Pallas kernels, on_device(): pl.pallas_call(value_kernel, out_shape=[shaped(DEVICES // 4, 17, 8, LANES...  8.2 us
    pallas_call x1, Pallas kernels, on_device(): pl.pallas_call(base_kernel, grid=(BLOCKS,), out_shape=[pltpu.HBM((BLOCKS,...  4.41 us
    pallas_call x1, Pallas kernels, on_device(): pl.pallas_call(tile_kernel, out_shape=[shaped(SCEN * LANES, 2 * LANES), s...  2.75 us
    pallas_call x1, Pallas kernels, on_device(): pl.pallas_call(send_kernel, out_shape=shaped(DEVICES * MSG1, LANES), in_s...  2.7 us
  transfers between devices with their start and end apart: 2, of which 2 were waited for; matrix products, arithmetic and copies ran while one was open for 0% of the time, Pallas kernels for 5%

profile of v3, /device:TPU:1, one launch (start us, length us, event | category | flops | bytes accessed | tf_op | source)
XLA Modules:
  0.0 106.5 jit_solution(11080458135434706608)
XLA Ops:
  0.6 0.0 copy-start.3
  0.6 0.0 copy-start.4
  0.7 2.7 %shard_map.120 = f32[2304,128]{1,0:T(8,128)} custom-call(s32[8,128]{1,0:T(8,128)} %bitcast.20, f32[128,1024]{1,0:T(8,128)} %coef_hbm.1, f32[8,128]{1,0:T(8,128)} %bitcast.22, f32[8,128]{1,0:T(8,128)} %bitcast.24, f32[2,128]{1,0:T(2,128)} %bitcast.27), custom_call_target="tpu_custom_call" | custom-call | tf_op jit(solution)/shard_map/pallas_call | solution.py:494
  3.4 11.9 %all-to-all-start = ((f32[128,9,2,128]{3,2,1,0:T(2,128)}), f32[128,9,2,128]{3,2,1,0:T(2,128)}, u32[]{:S(2)}, u32[]{:S(2)}) async-start(f32[128,9,2,128]{3,2,1,0:T(2,128)} %bitcast.30), calls=%async_computation | async-start | bytes 2359296 | tf_op jit(solution)/shard_map/all_to_all | solution.py:455
  15.3 0.0 copy-done.3
  15.3 0.0 copy-done.4
  15.3 4.4 %shard_map.121 = (f32[4,136,512]{2,1,0:T(8,128)}, bf16[2,1024,512]{2,1,0:T(8,128)(2,1)}, bf16[2,1024,512]{2,1,0:T(8,128)(2,1)}) custom-call(f32[1,2048]{1,0:T(1,128)S(1)} %copy-done.3, f32[1,2048]{1,0:T(1,128)S(1)} %copy-done.4), custom_call_target="tpu_custom_call" | custom-call | flops 4194304 | bytes 2097152 | tf_op jit(solution)/shard_map/pallas_call | solution.py:515
  19.7 14.9 %all-to-all-done = f32[128,9,2,128]{3,2,1,0:T(2,128)} async-done(((f32[128,9,2,128]{3,2,1,0:T(2,128)}), f32[128,9,2,128]{3,2,1,0:T(2,128)}, u32[]{:S(2)}, u32[]{:S(2)}) %all-to-all-start) | async-done | bytes 1179680 | tf_op jit(solution)/shard_map/all_to_all | solution.py:455
  34.6 8.2 %shard_map.122 = (f32[32,17,8,128]{3,2,1,0:T(8,128)}, f32[1]{0:T(128)}) custom-call(f32[2304,128]{1,0:T(8,128)} %bitcast.5.in_hbm, f32[4,136,512]{2,1,0:T(8,128)} %get-tuple-element.18.base_hbm, bf16[2,1024,512]{2,1,0:T(8,128)(2,1)} %get-tuple-element.19.hi_hbm, bf16[2,1024,512]{2,1,0:T(8,128)(2,1)} %get-tuple-element.20.low_hbm), custom_call_target="tpu_custom_call" | custom-call | tf_op jit(solution)/shard_map/pallas_call | solution.py:542
  42.9 0.0 copy-start
  42.9 0.0 copy-start.5
  42.9 0.0 copy-start.6
  42.9 5.1 %all-to-all-start.1 = ((f32[128,17,2,128]{3,2,1,0:T(2,128)}), f32[128,17,2,128]{3,2,1,0:T(2,128)S(1)}, u32[]{:S(2)}, u32[]{:S(2)}) async-start(f32[128,17,2,128]{3,2,1,0:T(2,128)} %bitcast.31), calls=%async_computation.1 | async-start | bytes 4456448 | tf_op jit(solution)/shard_map/all_to_all | solution.py:455
  48.0 0.0 copy-start.1
  48.0 0.0 copy-start.2
  48.7 0.6 shard_map.123.choice_ref
  49.3 31.6 %all-to-all-done.1 = f32[128,17,2,128]{3,2,1,0:T(2,128)S(1)} async-done(((f32[128,17,2,128]{3,2,1,0:T(2,128)}), f32[128,17,2,128]{3,2,1,0:T(2,128)S(1)}, u32[]{:S(2)}, u32[]{:S(2)}) %all-to-all-start.1) | async-done | bytes 2228256 | tf_op jit(solution)/shard_map/all_to_all | solution.py:455
  80.9 0.0 copy-done.6
  80.9 2.8 %shard_map.124 = (f32[1024,256]{1,0:T(8,128)S(1)}, f32[192,128]{1,0:T(8,128)S(1)}, f32[2,128]{1,0:T(2,128)S(1)}, f32[1024,256]{1,0:T(8,128)}) custom-call(f32[4352,128]{1,0:T(8,128)S(1)} %bitcast.17, bf16[8,128,256]{2,1,0:T(8,128)(2,1)S(1)} %shard_map.123.choice_ref, f32[2,128]{1,0:T(2,128)S(1)} %bitcast.28, f32[2,128]{1,0:T(2,128)S(1)} %bitcast.29, ...), custom_call_target="tpu_custom_call" | custom-call | tf_op jit(solution)/shard_map/pallas_call | solution.py:553
  83.7 7.6 %all_to_all.20 = f32[8,24,128]{2,1,0:T(8,128)S(1)} all-to-all(f32[8,24,128]{2,1,0:T(8,128)S(1)} %bitcast.19), channel_id=1, replica_groups=mesh['z_lo'=2,'x'=4,'z_hi'=2,'y'=4,'core'=2] {'x','z_lo'}, dimensions={0} | all-to-all | bytes 196608 | tf_op jit(solution)/shard_map/all_to_all | solution.py:455
  91.3 0.0 copy-done.1
  91.3 2.0 %shard_map.125 = (f32[8,128]{1,0:T(8,128)}, f32[32,128]{1,0:T(8,128)S(1)}, f32[1024,256]{1,0:T(8,128)}, f32[1]{0:T(128)}, f32[1]{0:T(128)}) custom-call(f32[192,128]{1,0:T(8,128)S(1)} %bitcast.18, f32[1024,256]{1,0:T(8,128)S(1)} %get-tuple-element.24.tile_ref, f32[8,128]{1,0:T(8,128)S(1)} %bitcast.23, ...), custom_call_target="tpu_custom_call", output_to_operand_aliasing={{2}: (4, {})} | custom-call | tf_op jit(solution)/shard_map/pallas_call | solution.py:568
  93.4 12.0 %all_to_all.21 = f32[16,2,128]{2,1,0:T(2,128)S(1)} all-to-all(f32[16,2,128]{2,1,0:T(2,128)S(1)} %bitcast.26), channel_id=1, replica_groups=mesh['z_lo'=2,'x'=4,'z_hi'=2,'y'=4,'core'=2] {'core','y','z_hi'}, dimensions={0} | all-to-all | bytes 32768 | tf_op jit(solution)/shard_map/all_to_all | solution.py:455
  105.3 1.2 %clamp_bitcast_fusion = f32[256]{0:T(256)} fusion(f32[2,128]{1,0:T(2,128)S(1)} %get-tuple-element.28, f32[2,128]{1,0:T(2,128)S(1)} %reduce_sum.9, f32[]{:T(128)} %bitcast.13, f32[256]{0:T(256)S(1)} %copy-done.6), kind=kLoop, calls=%fused_computation | loop fusion | flops 1536 | bytes 4100 | tf_op jit(solution)/shard_map/reshape | solution.py:586
  (4 shorter events, 0.0 us)
Async XLA Ops:
  0.6 14.6 %copy-start.3 = (f32[1,2048]{1,0:T(1,128)S(1)}, f32[1,2048]{1,0:T(1,128)}, u32[]{:S(2)}) copy-start(f32[1,2048]{1,0:T(1,128)} %mean_ref.1) | copy-start | bytes 24580
  0.6 14.6 %copy-start.4 = (f32[1,2048]{1,0:T(1,128)S(1)}, f32[1,2048]{1,0:T(1,128)}, u32[]{:S(2)}) copy-start(f32[1,2048]{1,0:T(1,128)} %spread_ref.1) | copy-start | bytes 24580
  3.4 31.3 %all-to-all-start = ((f32[128,9,2,128]{3,2,1,0:T(2,128)}), f32[128,9,2,128]{3,2,1,0:T(2,128)}, u32[]{:S(2)}, u32[]{:S(2)}) async-start(f32[128,9,2,128]{3,2,1,0:T(2,128)} %bitcast.30), calls=%async_computation | async-start | bytes 2359296 | tf_op jit(solution)/shard_map/all_to_all | solution.py:455
  42.9 5.9 %copy-start = (s32[1024,1]{0,1:T(1,128)S(1)}, s32[1024,1]{0,1:T(1,128)}, u32[]{:S(2)}) copy-start(s32[1024,1]{0,1:T(1,128)} %param.10) | copy-start | bytes 12292
  42.9 38.0 %copy-start.5 = (f32[256]{0:T(256)S(1)}, f32[256]{0:T(256)}, u32[]{:S(2)}) copy-start(f32[256]{0:T(256)} %param.16) | copy-start | bytes 3076
  42.9 38.0 %copy-start.6 = (f32[256]{0:T(256)S(1)}, f32[256]{0:T(256)}, u32[]{:S(2)}) copy-start(f32[256]{0:T(256)} %param.15) | copy-start | bytes 3076
  42.9 38.0 %all-to-all-start.1 = ((f32[128,17,2,128]{3,2,1,0:T(2,128)}), f32[128,17,2,128]{3,2,1,0:T(2,128)S(1)}, u32[]{:S(2)}, u32[]{:S(2)}) async-start(f32[128,17,2,128]{3,2,1,0:T(2,128)} %bitcast.31), calls=%async_computation.1 | async-start | bytes 4456448 | tf_op jit(solution)/shard_map/all_to_all | solution.py:455
  48.0 43.3 %copy-start.1 = (f32[1024]{0:T(1024)S(1)}, f32[1024]{0:T(1024)}, u32[]{:S(2)}) copy-start(f32[1024]{0:T(1024)} %param.13) | copy-start | bytes 12292
  48.0 43.3 %copy-start.2 = (f32[1024]{0:T(1024)S(1)}, f32[1024]{0:T(1024)}, u32[]{:S(2)}) copy-start(f32[1024]{0:T(1024)} %param.14) | copy-start | bytes 12292

commit v4 on v3

--- a/solution.py
+++ b/solution.py
@@ -26,7 +26,7 @@
 BASE = 32
 TABLE = 512
 BLOCKS = SCENARIOS // TABLE
-READY = 2
+READY = 3
 BASE_ROWS = 4 * BASE + 8
 PAIR = MOST * CHUNKS
 DUAL = PAIR + 1
@@ -34,10 +34,12 @@
 MSG2 = MOST * 16 + 2
 PAYLOAD = 24
 PARTS = 4
+OUT_TILES = (2, 2, 4, 2, 17, 8, LANES)
 STORED = 5
 AXES = ("z_lo", "x", "z_hi", "y", "core")
 SIZES = (2, 4, 2, 4, 2)
 SCEN_AXES, OPT_AXES = AXES[:2], AXES[2:]
+PLACES = ("z_hi", "z_lo", "y", "x", "core")
 F32 = jnp.float32
 BF16 = jnp.bfloat16
 HIGHEST = lax.Precision.HIGHEST
@@ -55,6 +57,17 @@
 
 def owner_of(place):
     return (place & (SCEN - 1)) * OPT + (place >> 3)
+
+
+def place_of(scen, opt):
+    (z_lo, x), (z_hi, rest) = divmod(scen, 4), divmod(opt, 8)
+    y, core = divmod(rest, 2)
+    return (((z_hi * 2 + z_lo) * 4 + y) * 4 + x) * 2 + core
+
+
+def underlying_at(place):
+    z_hi, z_lo, y, x = place >> 6, (place >> 5) & 1, (place >> 3) & 3, (place >> 1) & 3
+    return (z_lo * 4 + x) * OPT + z_hi * 8 + y * 2 + (place & 1)
 
 
 def mm(a, b, dims=NN):
@@ -210,7 +223,7 @@
         [own_ref[...].astype(F32), jnp.zeros((LANES - SCEN, LANES), F32)], axis=0
     ).T
     lower = (across < down).astype(F32).astype(BF16)
-    owner = across.astype(F32)
+    owner = underlying_at(across).astype(F32)
     for s in range(SCEN):
         same = names[:, s : s + 1] == owner
         before = mm(lower, same.astype(F32).astype(BF16))
@@ -243,14 +256,13 @@
 
 def value_kernel(
     in_hbm, base_hbm, hi_hbm, low_hbm, out_hbm, mass_ref,
-    in_ref, base_ref, hi_0, low_0, hi_1, low_1, hi_made, low_made, coef, values, grad, out_ref, sems, out_sems,
+    in_ref, base_ref, hi_0, low_0, hi_made, low_made, coef, values, grad, out_ref, sems, out_sems,
 ):
     width = 2 * LANES
     rows = MOST * LANES
     firsts = [
         pltpu.make_async_copy(base_hbm.at[READY], base_ref.at[0], sems.at[2, 0]),
         pltpu.make_async_copy(in_hbm, in_ref, sems.at[2, 1]),
-        pltpu.make_async_copy(base_hbm.at[READY + 1], base_ref.at[1], sems.at[3, 0]),
     ]
     for copy in firsts:
         copy.start()
@@ -277,7 +289,6 @@
                 part - hi.astype(F32)
             ).astype(BF16)
     grad[...] = jnp.zeros_like(grad)
-    firsts[2].wait()
 
     def multiply(block, hi_ref, low_ref):
         both = mm(coef[...], hi_ref[...])
@@ -290,19 +301,19 @@
             for half in range(2):
                 weights = in_ref[pl.ds((half * SCEN + s) * MSG1 + DUAL, 1), :]
                 total = total + tile[:, half * LANES : (half + 1) * LANES] * weights
-            start = s * OPT * MSG2
             for o in range(OPT):
+                start = place_of(s, o) * MSG2
                 for rank in range(MOST):
                     for half in range(2):
                         out_ref[
-                            pl.ds(start + o * MSG2 + (rank * 2 + half) * 8, 8), :
+                            pl.ds(start + (rank * 2 + half) * 8, 8), :
                         ] = tile[
                             rank * LANES + o * 8 : rank * LANES + o * 8 + 8,
                             half * LANES : (half + 1) * LANES,
                         ]
         grad[...] = total
 
-    tiles = out_ref.reshape(DEVICES // 4, 17, 8, LANES)
+    tiles = out_ref.reshape(OUT_TILES)
     outs = []
 
     def send(*view):
@@ -312,15 +323,12 @@
         outs[-1].start()
 
     def send_values(block):
-        share = DEVICES // 4 // BLOCKS
+        every, (z_lo, x_pair) = slice(None), divmod(block, 2)
         for first, last in ((0, 4), (5, 8), (9, 12), (13, 16)):
-            send(slice(block * share, (block + 1) * share), slice(first, last))
+            send(every, z_lo, every, x_pair, slice(first, last))
 
     multiply(READY, hi_0, low_0)
     send_values(READY)
-    table(base_ref.at[1], hi_1, low_1)
-    multiply(READY + 1, hi_1, low_1)
-    send_values(READY + 1)
     for block in range(READY):
         for copy in copies[block]:
             copy.wait()
@@ -344,11 +352,12 @@
     for s in range(SCEN):
         for half in range(2):
             pnl = values[s, :, half * LANES : (half + 1) * LANES] * bar
-            out_ref[pl.ds(s * OPT * MSG2 + MSG2 - 2 + half, OPT, stride=MSG2), :] = (
-                jnp.broadcast_to(jnp.sum(pnl, axis=0, keepdims=True), (OPT, LANES))
-            )
+            pnl = jnp.broadcast_to(jnp.sum(pnl, axis=0, keepdims=True), (4, LANES))
+            for o in (0, 1, 8, 9):
+                first = place_of(s, o) * MSG2 + MSG2 - 2 + half
+                out_ref[pl.ds(first, 4, stride=8 * MSG2), :] = pnl
     for tile in (4, 8, 12, 16):
-        send(slice(0, DEVICES // 4), slice(tile, tile + 1))
+        send(*[slice(None)] * 4, slice(tile, tile + 1))
     for out in outs:
         out.wait()
 
@@ -463,13 +472,13 @@
     return [
         pltpu.VMEM((DEVICES * MSG1, LANES), F32),
         pltpu.VMEM((BLOCKS - READY, BASE_ROWS, TABLE), F32),
-        *[pltpu.VMEM((TERMS, TABLE), BF16)] * 4,
+        *[pltpu.VMEM((TERMS, TABLE), BF16)] * 2,
         *[pltpu.VMEM((READY, TERMS, TABLE), BF16)] * 2,
         pltpu.VMEM((2 * MOST * LANES, TERMS), BF16),
         pltpu.VMEM((SCEN, MOST * LANES, 2 * LANES), F32),
         pltpu.VMEM((MOST * LANES, LANES), F32),
         pltpu.VMEM((DEVICES * MSG2, LANES), F32),
-        pltpu.SemaphoreType.DMA((4, 2)),
+        pltpu.SemaphoreType.DMA((4, READY)),
         pltpu.SemaphoreType.DMA((4 * BLOCKS + 4,)),
     ]
 
@@ -541,13 +550,13 @@
 
     values, mass = pl.pallas_call(
         value_kernel,
-        out_shape=[shaped(DEVICES // 4, 17, 8, LANES), shaped(1)],
+        out_shape=[shaped(*OUT_TILES), shaped(1)],
         in_specs=[HBM] * 4,
         out_specs=[HBM, SMEM],
         scratch_shapes=value_scratch(),
         compiler_params=params(63),
     )(got, base, made_hi, made_low)
-    arrived = exchange(values.reshape(DEVICES, MSG2 // 2, 2, LANES), AXES)
+    arrived = exchange(values.reshape(DEVICES, MSG2 // 2, 2, LANES), PLACES)
     arrived = arrived.reshape(DEVICES * MSG2, LANES)
 
     tile, payload, first_duals, kept = pl.pallas_call(

time: 107 us -> 106 us (level)
  waiting for transfers between devices: 46.5 us -> 44.7 us
    all_to_all x2, waiting for transfers between devices: 46.5 us -> 44.7 us  [exchange(): return lax.all_to_all(x, axes, split_axis=0, concat_axis=0, tiled=True)]
  transfers between devices with their start and end apart: 2 -> 2, of which waited for: 2 -> 2; matrix products, arithmetic and copies ran while one was open for 0% -> 0% of each run, Pallas kernels for 5% -> 6%
where the time goes in v4:
time: 106 us; the launch traced here: 105 us
  waiting for transfers between devices  44.7 us (42%)
  Pallas kernels  21.1 us (20%)
  blocking collectives  19.8 us (19%)
  starting transfers between devices  17 us (16%)
  between operations  1.43 us (1%)
  other arithmetic  1.23 us (1%)
    all_to_all x2, waiting for transfers between devices, exchange(): return lax.all_to_all(x, axes, split_axis=0, concat_axis=0, tiled=True)  44.7 us
    all_to_all x2, blocking collectives, exchange(): return lax.all_to_all(x, axes, split_axis=0, concat_axis=0, tiled=True)  19.8 us
    all_to_all x2, starting transfers between devices, exchange(): return lax.all_to_all(x, axes, split_axis=0, concat_axis=0, tiled=True)  17 us
    pallas_call x1, Pallas kernels, on_device(): pl.pallas_call(value_kernel, out_shape=[shaped(*OUT_TILES), shaped(1)], i...  7.77 us
    pallas_call x1, Pallas kernels, on_device(): pl.pallas_call(base_kernel, grid=(BLOCKS,), out_shape=[pltpu.HBM((BLOCKS,...  5.25 us
    pallas_call x1, Pallas kernels, on_device(): pl.pallas_call(tile_kernel, out_shape=[shaped(SCEN * LANES, 2 * LANES), s...  2.76 us
    pallas_call x1, Pallas kernels, on_device(): pl.pallas_call(send_kernel, out_shape=shaped(DEVICES * MSG1, LANES), in_s...  2.72 us
  transfers between devices with their start and end apart: 2, of which 2 were waited for; matrix products, arithmetic and copies ran while one was open for 0% of the time, Pallas kernels for 6%

profile of v4, /device:TPU:1, one launch (start us, length us, event | category | flops | bytes accessed | tf_op | source)
XLA Modules:
  0.0 105.4 jit_solution(11050844212053958159)
XLA Ops:
  0.6 0.0 copy-start.3
  0.6 0.0 copy-start.4
  0.7 2.7 %shard_map.120 = f32[2304,128]{1,0:T(8,128)} custom-call(s32[8,128]{1,0:T(8,128)} %bitcast.20, f32[128,1024]{1,0:T(8,128)} %coef_hbm.1, f32[8,128]{1,0:T(8,128)} %bitcast.22, f32[8,128]{1,0:T(8,128)} %bitcast.24, f32[2,128]{1,0:T(2,128)} %bitcast.27), custom_call_target="tpu_custom_call" | custom-call | tf_op jit(solution)/shard_map/pallas_call | solution.py:503
  3.4 11.9 %all-to-all-start = ((f32[128,9,2,128]{3,2,1,0:T(2,128)}), f32[128,9,2,128]{3,2,1,0:T(2,128)}, u32[]{:S(2)}, u32[]{:S(2)}) async-start(f32[128,9,2,128]{3,2,1,0:T(2,128)} %bitcast.30), calls=%async_computation | async-start | bytes 2359296 | tf_op jit(solution)/shard_map/all_to_all | solution.py:464
  15.3 0.0 copy-done.3
  15.3 0.0 copy-done.4
  15.3 5.3 %shard_map.121 = (f32[4,136,512]{2,1,0:T(8,128)}, bf16[3,1024,512]{2,1,0:T(8,128)(2,1)}, bf16[3,1024,512]{2,1,0:T(8,128)(2,1)}) custom-call(f32[1,2048]{1,0:T(1,128)S(1)} %copy-done.3, f32[1,2048]{1,0:T(1,128)S(1)} %copy-done.4), custom_call_target="tpu_custom_call" | custom-call | flops 4194304 | bytes 2097152 | tf_op jit(solution)/shard_map/pallas_call | solution.py:524
  20.6 14.1 %all-to-all-done = f32[128,9,2,128]{3,2,1,0:T(2,128)} async-done(((f32[128,9,2,128]{3,2,1,0:T(2,128)}), f32[128,9,2,128]{3,2,1,0:T(2,128)}, u32[]{:S(2)}, u32[]{:S(2)}) %all-to-all-start) | async-done | bytes 1179680 | tf_op jit(solution)/shard_map/all_to_all | solution.py:464
  34.7 7.8 %shard_map.122 = (f32[2,2,4,2,17,8,128]{6,5,4,3,2,1,0:T(8,128)}, f32[1]{0:T(128)}) custom-call(f32[2304,128]{1,0:T(8,128)} %bitcast.5.in_hbm, f32[4,136,512]{2,1,0:T(8,128)} %get-tuple-element.18.base_hbm, bf16[3,1024,512]{2,1,0:T(8,128)(2,1)} %get-tuple-element.19.hi_hbm, bf16[3,1024,512]{2,1,0:T(8,128)(2,1)} %get-tuple-element.20.low_hbm), custom_call_target="tpu_custom_call" | custom-call | tf_op jit(solution)/shard_map/pallas_call | solution.py:551
  42.4 0.0 copy-start
  42.5 0.0 copy-start.5
  42.5 0.0 copy-start.6
  42.5 5.1 %all-to-all-start.1 = ((f32[128,17,2,128]{3,2,1,0:T(2,128)}), f32[128,17,2,128]{3,2,1,0:T(2,128)S(1)}, u32[]{:S(2)}, u32[]{:S(2)}) async-start(f32[128,17,2,128]{3,2,1,0:T(2,128)} %bitcast.31), calls=%async_computation.1 | async-start | bytes 4456448 | tf_op jit(solution)/shard_map/all_to_all | solution.py:464
  47.6 0.0 copy-start.1
  47.6 0.0 copy-start.2
  48.3 0.6 shard_map.123.choice_ref
  48.9 30.6 %all-to-all-done.1 = f32[128,17,2,128]{3,2,1,0:T(2,128)S(1)} async-done(((f32[128,17,2,128]{3,2,1,0:T(2,128)}), f32[128,17,2,128]{3,2,1,0:T(2,128)S(1)}, u32[]{:S(2)}, u32[]{:S(2)}) %all-to-all-start.1) | async-done | bytes 2228256 | tf_op jit(solution)/shard_map/all_to_all | solution.py:464
  79.5 0.0 copy-done.5
  79.5 2.8 %shard_map.124 = (f32[1024,256]{1,0:T(8,128)S(1)}, f32[192,128]{1,0:T(8,128)S(1)}, f32[2,128]{1,0:T(2,128)S(1)}, f32[1024,256]{1,0:T(8,128)}) custom-call(f32[4352,128]{1,0:T(8,128)S(1)} %bitcast.17, bf16[8,128,256]{2,1,0:T(8,128)(2,1)S(1)} %shard_map.123.choice_ref, f32[2,128]{1,0:T(2,128)S(1)} %bitcast.28, f32[2,128]{1,0:T(2,128)S(1)} %bitcast.29, ...), custom_call_target="tpu_custom_call" | custom-call | tf_op jit(solution)/shard_map/pallas_call | solution.py:562
  82.3 7.5 %all_to_all.20 = f32[8,24,128]{2,1,0:T(8,128)S(1)} all-to-all(f32[8,24,128]{2,1,0:T(8,128)S(1)} %bitcast.19), channel_id=1, replica_groups=mesh['z_lo'=2,'x'=4,'z_hi'=2,'y'=4,'core'=2] {'x','z_lo'}, dimensions={0} | all-to-all | bytes 196608 | tf_op jit(solution)/shard_map/all_to_all | solution.py:464
  89.8 0.0 copy-done.2
  89.8 2.0 %shard_map.125 = (f32[8,128]{1,0:T(8,128)}, f32[32,128]{1,0:T(8,128)S(1)}, f32[1024,256]{1,0:T(8,128)}, f32[1]{0:T(128)}, f32[1]{0:T(128)}) custom-call(f32[192,128]{1,0:T(8,128)S(1)} %bitcast.18, f32[1024,256]{1,0:T(8,128)S(1)} %get-tuple-element.24.tile_ref, f32[8,128]{1,0:T(8,128)S(1)} %bitcast.23, ...), custom_call_target="tpu_custom_call", output_to_operand_aliasing={{2}: (4, {})} | custom-call | tf_op jit(solution)/shard_map/pallas_call | solution.py:577
  91.9 12.3 %all_to_all.21 = f32[16,2,128]{2,1,0:T(2,128)S(1)} all-to-all(f32[16,2,128]{2,1,0:T(2,128)S(1)} %bitcast.26), channel_id=1, replica_groups=mesh['z_lo'=2,'x'=4,'z_hi'=2,'y'=4,'core'=2] {'core','y','z_hi'}, dimensions={0} | all-to-all | bytes 32768 | tf_op jit(solution)/shard_map/all_to_all | solution.py:464
  104.2 1.2 %clamp_bitcast_fusion = f32[256]{0:T(256)} fusion(f32[2,128]{1,0:T(2,128)S(1)} %get-tuple-element.28, f32[2,128]{1,0:T(2,128)S(1)} %reduce_sum.9, f32[]{:T(128)} %bitcast.13, f32[256]{0:T(256)S(1)} %copy-done.6), kind=kLoop, calls=%fused_computation | loop fusion | flops 1536 | bytes 4100 | tf_op jit(solution)/shard_map/reshape | solution.py:595
  (4 shorter events, 0.0 us)
Async XLA Ops:
  0.6 14.7 %copy-start.3 = (f32[1,2048]{1,0:T(1,128)S(1)}, f32[1,2048]{1,0:T(1,128)}, u32[]{:S(2)}) copy-start(f32[1,2048]{1,0:T(1,128)} %mean_ref.1) | copy-start | bytes 24580
  0.6 14.7 %copy-start.4 = (f32[1,2048]{1,0:T(1,128)S(1)}, f32[1,2048]{1,0:T(1,128)}, u32[]{:S(2)}) copy-start(f32[1,2048]{1,0:T(1,128)} %spread_ref.1) | copy-start | bytes 24580
  3.4 31.3 %all-to-all-start = ((f32[128,9,2,128]{3,2,1,0:T(2,128)}), f32[128,9,2,128]{3,2,1,0:T(2,128)}, u32[]{:S(2)}, u32[]{:S(2)}) async-start(f32[128,9,2,128]{3,2,1,0:T(2,128)} %bitcast.30), calls=%async_computation | async-start | bytes 2359296 | tf_op jit(solution)/shard_map/all_to_all | solution.py:464
  42.4 5.9 %copy-start = (s32[1024,1]{0,1:T(1,128)S(1)}, s32[1024,1]{0,1:T(1,128)}, u32[]{:S(2)}) copy-start(s32[1024,1]{0,1:T(1,128)} %param.10) | copy-start | bytes 12292
  42.5 37.1 %copy-start.5 = (f32[256]{0:T(256)S(1)}, f32[256]{0:T(256)}, u32[]{:S(2)}) copy-start(f32[256]{0:T(256)} %param.16) | copy-start | bytes 3076
  42.5 37.0 %copy-start.6 = (f32[256]{0:T(256)S(1)}, f32[256]{0:T(256)}, u32[]{:S(2)}) copy-start(f32[256]{0:T(256)} %param.15) | copy-start | bytes 3076
  42.5 37.0 %all-to-all-start.1 = ((f32[128,17,2,128]{3,2,1,0:T(2,128)}), f32[128,17,2,128]{3,2,1,0:T(2,128)S(1)}, u32[]{:S(2)}, u32[]{:S(2)}) async-start(f32[128,17,2,128]{3,2,1,0:T(2,128)} %bitcast.31), calls=%async_computation.1 | async-start | bytes 4456448 | tf_op jit(solution)/shard_map/all_to_all | solution.py:464
  47.6 42.2 %copy-start.1 = (f32[1024]{0:T(1024)S(1)}, f32[1024]{0:T(1024)}, u32[]{:S(2)}) copy-start(f32[1024]{0:T(1024)} %param.13) | copy-start | bytes 12292
  47.6 42.2 %copy-start.2 = (f32[1024]{0:T(1024)S(1)}, f32[1024]{0:T(1024)}, u32[]{:S(2)}) copy-start(f32[1024]{0:T(1024)} %param.14) | copy-start | bytes 12292

commit v5 on v4

--- a/solution.py
+++ b/solution.py
@@ -216,7 +216,9 @@
         table(out_ref.at[0], hi_ref.at[0], low_ref.at[0])
 
 
-def choice_kernel(own_ref, out_ref):
+def choice_kernel(own_ref, in_hbm, out_ref, mass_ref, in_ref, sem):
+    first = pltpu.make_async_copy(in_hbm.at[0 : 2 * SCEN * MSG1], in_ref, sem)
+    first.start()
     square = (LANES, LANES)
     down, across = iota(square, 0), iota(square, 1)
     names = jnp.concatenate(
@@ -231,6 +233,12 @@
             out_ref[s, :, rank * LANES : (rank + 1) * LANES] = jnp.where(
                 same & (before == float(rank)), 1.0, 0.0
             ).astype(BF16)
+    first.wait()
+    mass = jnp.zeros((1, LANES), F32)
+    for place in range(2 * SCEN):
+        at = place * MSG1 + DUAL
+        mass = mass + in_ref[at : at + 1, :]
+    mass_ref[0] = jnp.sum(mass)
 
 
 def table(base_ref, hi_ref, low_ref):
@@ -255,7 +263,7 @@
 
 
 def value_kernel(
-    in_hbm, base_hbm, hi_hbm, low_hbm, out_hbm, mass_ref,
+    in_hbm, base_hbm, hi_hbm, low_hbm, out_hbm,
     in_ref, base_ref, hi_0, low_0, hi_made, low_made, coef, values, grad, out_ref, sems, out_sems,
 ):
     width = 2 * LANES
@@ -335,11 +343,6 @@
         multiply(block, hi_made.at[block], low_made.at[block])
         send_values(block)
 
-    mass = jnp.zeros((1, LANES), F32)
-    for place in range(2 * SCEN):
-        at = place * MSG1 + DUAL
-        mass = mass + in_ref[at : at + 1, :]
-    mass_ref[0] = jnp.sum(mass)
     extra = in_ref[pl.ds(PAIR, DEVICES, stride=MSG1), :]
     bars = []
     for rank in range(MOST):
@@ -423,7 +426,7 @@
 
 def position_kernel(
     in_ref, tile_ref, cost_ref, pos_ref, kept_ref, mass_ref, level_ref,
-    pos_out, pnl_out, tile_hbm, level_out, bar_out, sem,
+    pos_out, pnl_out, bar_out, tile_hbm, level_out, sem,
 ):
     rest = slice(STORED * LANES, SCEN * LANES)
     keep = pltpu.make_async_copy(tile_ref.at[rest], tile_hbm.at[rest], sem)
@@ -434,7 +437,7 @@
     level = level_step(level_ref[0], mass_ref[0])
     later = level_step(level, jnp.sum(total[16:17, :]))
     level_out[0] = later
-    bar_out[0] = 2.0 * later - level
+    bar_out[...] = jnp.full(bar_out.shape, 2.0 * later - level, F32)
     cost = cost_ref[...]
     first = primal(pos_ref[...], cost, total[0:8, :])
     second = primal(first, cost, total[8:16, :])
@@ -537,22 +540,26 @@
             transcendentals=0,
         ),
     )(log_return_mean, log_return_spread)
-    choice = pl.pallas_call(
+    choice, mass = pl.pallas_call(
         choice_kernel,
-        out_shape=shaped(SCEN, LANES, MOST * LANES, dtype=BF16),
-        in_specs=[VMEM],
-        out_specs=VMEM,
+        out_shape=[shaped(SCEN, LANES, MOST * LANES, dtype=BF16), shaped(1)],
+        in_specs=[VMEM, HBM],
+        out_specs=[VMEM, SMEM],
+        scratch_shapes=[
+            pltpu.VMEM((2 * SCEN * MSG1, LANES), F32),
+            pltpu.SemaphoreType.DMA(()),
+        ],
         compiler_params=params(4),
         cost_estimate=pl.CostEstimate(
             flops=TERMS * SCENARIOS, bytes_accessed=SCENARIOS, transcendentals=0
         ),
-    )(own)
-
-    values, mass = pl.pallas_call(
+    )(own, got)
+
+    values = pl.pallas_call(
         value_kernel,
-        out_shape=[shaped(*OUT_TILES), shaped(1)],
+        out_shape=shaped(*OUT_TILES),
         in_specs=[HBM] * 4,
-        out_specs=[HBM, SMEM],
+        out_specs=HBM,
         scratch_shapes=value_scratch(),
         compiler_params=params(63),
     )(got, base, made_hi, made_low)
@@ -574,18 +581,18 @@
     )(arrived, choice, duals, base_loss, mass, threshold)
     gathered = exchange(payload.reshape(SCEN, PAYLOAD, LANES), SCEN_AXES[::-1])
 
-    new_positions, part_pnl, kept, level, level_bar = pl.pallas_call(
+    new_positions, part_pnl, level_bar, kept, level = pl.pallas_call(
         position_kernel,
         out_shape=[
             shaped(SCEN, LANES),
             shaped(OPT * 2, LANES),
+            shaped(2, LANES),
             shaped(SCEN * LANES, 2 * LANES),
-            shaped(1),
             shaped(1),
         ],
         in_specs=[VMEM] * 4 + [HBM] + [SMEM] * 2,
-        out_specs=[VMEM] * 2 + [HBM] + [SMEM] * 2,
-        input_output_aliases={4: 2},
+        out_specs=[VMEM] * 3 + [HBM, SMEM],
+        input_output_aliases={4: 3},
         scratch_shapes=[pltpu.SemaphoreType.DMA(())],
         compiler_params=params(8),
     )(gathered.reshape(SCEN * PAYLOAD, LANES), tile, cost, positions, kept, mass, threshold)

time: 106 us -> 105 us (level)
  transfers between devices with their start and end apart: 2 -> 2, of which waited for: 2 -> 2; matrix products, arithmetic and copies ran while one was open for 0% -> 0% of each run, Pallas kernels for 6% -> 7%
where the time goes in v5:
time: 105 us; the launch traced here: 104 us
  waiting for transfers between devices  43.7 us (42%)
  Pallas kernels  21.6 us (21%)
  blocking collectives  19.8 us (19%)
  starting transfers between devices  17 us (16%)
  between operations  1.43 us (1%)
    all_to_all x2, waiting for transfers between devices, exchange(): return lax.all_to_all(x, axes, split_axis=0, concat_axis=0, tiled=True)  43.7 us
    all_to_all x2, blocking collectives, exchange(): return lax.all_to_all(x, axes, split_axis=0, concat_axis=0, tiled=True)  19.8 us
    all_to_all x2, starting transfers between devices, exchange(): return lax.all_to_all(x, axes, split_axis=0, concat_axis=0, tiled=True)  17 us
    pallas_call x1, Pallas kernels, on_device(): pl.pallas_call(value_kernel, out_shape=shaped(*OUT_TILES), in_specs=[HBM]...  7.26 us
    pallas_call x1, Pallas kernels, on_device(): pl.pallas_call(base_kernel, grid=(BLOCKS,), out_shape=[pltpu.HBM((BLOCKS,...  5.25 us
    pallas_call x1, Pallas kernels, on_device(): pl.pallas_call(tile_kernel, out_shape=[shaped(SCEN * LANES, 2 * LANES), s...  2.76 us
    pallas_call x1, Pallas kernels, on_device(): pl.pallas_call(send_kernel, out_shape=shaped(DEVICES * MSG1, LANES), in_s...  2.72 us
  transfers between devices with their start and end apart: 2, of which 2 were waited for; matrix products, arithmetic and copies ran while one was open for 0% of the time, Pallas kernels for 7%

profile of v5, /device:TPU:1, one launch (start us, length us, event | category | flops | bytes accessed | tf_op | source)
XLA Modules:
  0.0 104.2 jit_solution(15802118324846121790)
XLA Ops:
  0.6 0.0 copy-start.3
  0.6 0.0 copy-start.4
  0.7 2.7 %shard_map.120 = f32[2304,128]{1,0:T(8,128)} custom-call(s32[8,128]{1,0:T(8,128)} %bitcast.19, f32[128,1024]{1,0:T(8,128)} %coef_hbm.1, f32[8,128]{1,0:T(8,128)} %bitcast.21, f32[8,128]{1,0:T(8,128)} %bitcast.23, f32[2,128]{1,0:T(2,128)} %bitcast.26), custom_call_target="tpu_custom_call" | custom-call | tf_op jit(solution)/shard_map/pallas_call | solution.py:506
  3.4 11.9 %all-to-all-start = ((f32[128,9,2,128]{3,2,1,0:T(2,128)}), f32[128,9,2,128]{3,2,1,0:T(2,128)}, u32[]{:S(2)}, u32[]{:S(2)}) async-start(f32[128,9,2,128]{3,2,1,0:T(2,128)} %bitcast.30), calls=%async_computation | async-start | bytes 2359296 | tf_op jit(solution)/shard_map/all_to_all | solution.py:467
  15.3 0.0 copy-done.3
  15.3 0.0 copy-done.4
  15.3 5.3 %shard_map.121 = (f32[4,136,512]{2,1,0:T(8,128)}, bf16[3,1024,512]{2,1,0:T(8,128)(2,1)}, bf16[3,1024,512]{2,1,0:T(8,128)(2,1)}) custom-call(f32[1,2048]{1,0:T(1,128)S(1)} %copy-done.3, f32[1,2048]{1,0:T(1,128)S(1)} %copy-done.4), custom_call_target="tpu_custom_call" | custom-call | flops 4194304 | bytes 2097152 | tf_op jit(solution)/shard_map/pallas_call | solution.py:527
  20.6 14.1 %all-to-all-done = f32[128,9,2,128]{3,2,1,0:T(2,128)} async-done(((f32[128,9,2,128]{3,2,1,0:T(2,128)}), f32[128,9,2,128]{3,2,1,0:T(2,128)}, u32[]{:S(2)}, u32[]{:S(2)}) %all-to-all-start) | async-done | bytes 1179680 | tf_op jit(solution)/shard_map/all_to_all | solution.py:467
  34.7 7.3 %shard_map.122 = f32[2,2,4,2,17,8,128]{6,5,4,3,2,1,0:T(8,128)} custom-call(f32[2304,128]{1,0:T(8,128)} %bitcast.5.in_hbm, f32[4,136,512]{2,1,0:T(8,128)} %get-tuple-element.18.base_hbm, bf16[3,1024,512]{2,1,0:T(8,128)(2,1)} %get-tuple-element.19.hi_hbm, bf16[3,1024,512]{2,1,0:T(8,128)(2,1)} %get-tuple-element.20.low_hbm), custom_call_target="tpu_custom_call" | custom-call | tf_op jit(solution)/shard_map/pallas_call | solution.py:558
  41.9 0.0 copy-start
  41.9 0.0 copy-start.5
  41.9 0.0 copy-start.6
  42.0 5.1 %all-to-all-start.1 = ((f32[128,17,2,128]{3,2,1,0:T(2,128)}), f32[128,17,2,128]{3,2,1,0:T(2,128)S(1)}, u32[]{:S(2)}, u32[]{:S(2)}) async-start(f32[128,17,2,128]{3,2,1,0:T(2,128)} %bitcast.29), calls=%async_computation.1 | async-start | bytes 4456448 | tf_op jit(solution)/shard_map/all_to_all | solution.py:467
  47.1 0.0 copy-start.1
  47.1 0.0 copy-start.2
  47.8 0.0 copy-done
  47.8 1.6 %shard_map.123 = (bf16[8,128,256]{2,1,0:T(8,128)(2,1)S(1)}, f32[1]{0:T(128)}) custom-call(s32[8,128]{1,0:T(8,128)S(1)} %bitcast.20, f32[2304,128]{1,0:T(8,128)} %bitcast.5.in_hbm), custom_call_target="tpu_custom_call" | custom-call | flops 2097152 | bytes 2048 | tf_op jit(solution)/shard_map/pallas_call | solution.py:543
  49.4 29.6 %all-to-all-done.1 = f32[128,17,2,128]{3,2,1,0:T(2,128)S(1)} async-done(((f32[128,17,2,128]{3,2,1,0:T(2,128)}), f32[128,17,2,128]{3,2,1,0:T(2,128)S(1)}, u32[]{:S(2)}, u32[]{:S(2)}) %all-to-all-start.1) | async-done | bytes 2228256 | tf_op jit(solution)/shard_map/all_to_all | solution.py:467
  79.0 0.0 copy-done.5
  79.0 2.8 %shard_map.124 = (f32[1024,256]{1,0:T(8,128)S(1)}, f32[192,128]{1,0:T(8,128)S(1)}, f32[2,128]{1,0:T(2,128)S(1)}, f32[1024,256]{1,0:T(8,128)}) custom-call(f32[4352,128]{1,0:T(8,128)S(1)} %bitcast.16, bf16[8,128,256]{2,1,0:T(8,128)(2,1)S(1)} %get-tuple-element.21.choice_ref, f32[2,128]{1,0:T(2,128)S(1)} %bitcast.27, f32[2,128]{1,0:T(2,128)S(1)} %bitcast.28, ...), custom_call_target="tpu_custom_call" | custom-call | tf_op jit(solution)/shard_map/pallas_call | solution.py:569
  81.8 7.5 %all_to_all.20 = f32[8,24,128]{2,1,0:T(8,128)S(1)} all-to-all(f32[8,24,128]{2,1,0:T(8,128)S(1)} %bitcast.18), channel_id=1, replica_groups=mesh['z_lo'=2,'x'=4,'z_hi'=2,'y'=4,'core'=2] {'x','z_lo'}, dimensions={0} | all-to-all | bytes 196608 | tf_op jit(solution)/shard_map/all_to_all | solution.py:467
  89.3 2.0 %shard_map.125 = (f32[8,128]{1,0:T(8,128)}, f32[32,128]{1,0:T(8,128)S(1)}, f32[2,128]{1,0:T(2,128)S(1)}, f32[1024,256]{1,0:T(8,128)}, f32[1]{0:T(128)}) custom-call(f32[192,128]{1,0:T(8,128)S(1)} %bitcast.17, f32[1024,256]{1,0:T(8,128)S(1)} %get-tuple-element.24.tile_ref, f32[8,128]{1,0:T(8,128)S(1)} %bitcast.22, ...), custom_call_target="tpu_custom_call", output_to_operand_aliasing={{3}: (4, {})} | custom-call | tf_op jit(solution)/shard_map/pallas_call | solution.py:584
  91.3 12.3 %all_to_all.21 = f32[16,2,128]{2,1,0:T(2,128)S(1)} all-to-all(f32[16,2,128]{2,1,0:T(2,128)S(1)} %bitcast.25), channel_id=1, replica_groups=mesh['z_lo'=2,'x'=4,'z_hi'=2,'y'=4,'core'=2] {'core','y','z_hi'}, dimensions={0} | all-to-all | bytes 32768 | tf_op jit(solution)/shard_map/all_to_all | solution.py:467
  103.7 0.6 clamp_bitcast_fusion
  (4 shorter events, 0.0 us)
Async XLA Ops:
  0.6 14.7 %copy-start.3 = (f32[1,2048]{1,0:T(1,128)S(1)}, f32[1,2048]{1,0:T(1,128)}, u32[]{:S(2)}) copy-start(f32[1,2048]{1,0:T(1,128)} %mean_ref.1) | copy-start | bytes 24580
  0.6 14.7 %copy-start.4 = (f32[1,2048]{1,0:T(1,128)S(1)}, f32[1,2048]{1,0:T(1,128)}, u32[]{:S(2)}) copy-start(f32[1,2048]{1,0:T(1,128)} %spread_ref.1) | copy-start | bytes 24580
  3.4 31.3 %all-to-all-start = ((f32[128,9,2,128]{3,2,1,0:T(2,128)}), f32[128,9,2,128]{3,2,1,0:T(2,128)}, u32[]{:S(2)}, u32[]{:S(2)}) async-start(f32[128,9,2,128]{3,2,1,0:T(2,128)} %bitcast.30), calls=%async_computation | async-start | bytes 2359296 | tf_op jit(solution)/shard_map/all_to_all | solution.py:467
  41.9 5.9 %copy-start = (s32[1024,1]{0,1:T(1,128)S(1)}, s32[1024,1]{0,1:T(1,128)}, u32[]{:S(2)}) copy-start(s32[1024,1]{0,1:T(1,128)} %param.10) | copy-start | bytes 12292
  41.9 37.1 %copy-start.5 = (f32[256]{0:T(256)S(1)}, f32[256]{0:T(256)}, u32[]{:S(2)}) copy-start(f32[256]{0:T(256)} %param.16) | copy-start | bytes 3076
  41.9 37.0 %copy-start.6 = (f32[256]{0:T(256)S(1)}, f32[256]{0:T(256)}, u32[]{:S(2)}) copy-start(f32[256]{0:T(256)} %param.15) | copy-start | bytes 3076
  42.0 37.0 %all-to-all-start.1 = ((f32[128,17,2,128]{3,2,1,0:T(2,128)}), f32[128,17,2,128]{3,2,1,0:T(2,128)S(1)}, u32[]{:S(2)}, u32[]{:S(2)}) async-start(f32[128,17,2,128]{3,2,1,0:T(2,128)} %bitcast.29), calls=%async_computation.1 | async-start | bytes 4456448 | tf_op jit(solution)/shard_map/all_to_all | solution.py:467
  47.1 42.2 %copy-start.1 = (f32[1024]{0:T(1024)S(1)}, f32[1024]{0:T(1024)}, u32[]{:S(2)}) copy-start(f32[1024]{0:T(1024)} %param.13) | copy-start | bytes 12292
  47.1 42.2 %copy-start.2 = (f32[1024]{0:T(1024)S(1)}, f32[1024]{0:T(1024)}, u32[]{:S(2)}) copy-start(f32[1024]{0:T(1024)} %param.14) | copy-start | bytes 12292

commit v6 on v5

--- a/solution.py
+++ b/solution.py
@@ -33,7 +33,7 @@
 MSG1 = PAIR + 2
 MSG2 = MOST * 16 + 2
 PAYLOAD = 24
-PARTS = 4
+PARTS = 2
 OUT_TILES = (2, 2, 4, 2, 17, 8, LANES)
 STORED = 5
 AXES = ("z_lo", "x", "z_hi", "y", "core")

time: 105 us -> 105 us (level)
  no operation moved by 1% of the time
where the time goes in v6:
time: 105 us; the launch traced here: 104 us
  waiting for transfers between devices  43.7 us (42%)
  Pallas kernels  21.5 us (20%)
  blocking collectives  19.8 us (19%)
  starting transfers between devices  17 us (16%)
  between operations  1.43 us (1%)
    all_to_all x2, waiting for transfers between devices, exchange(): return lax.all_to_all(x, axes, split_axis=0, concat_axis=0, tiled=True)  43.7 us
    all_to_all x2, blocking collectives, exchange(): return lax.all_to_all(x, axes, split_axis=0, concat_axis=0, tiled=True)  19.8 us
    all_to_all x2, starting transfers between devices, exchange(): return lax.all_to_all(x, axes, split_axis=0, concat_axis=0, tiled=True)  17 us
    pallas_call x1, Pallas kernels, on_device(): pl.pallas_call(value_kernel, out_shape=shaped(*OUT_TILES), in_specs=[HBM]...  7.26 us
    pallas_call x1, Pallas kernels, on_device(): pl.pallas_call(base_kernel, grid=(BLOCKS,), out_shape=[pltpu.HBM((BLOCKS,...  5.25 us
    pallas_call x1, Pallas kernels, on_device(): pl.pallas_call(tile_kernel, out_shape=[shaped(SCEN * LANES, 2 * LANES), s...  2.75 us
    pallas_call x1, Pallas kernels, on_device(): pl.pallas_call(send_kernel, out_shape=shaped(DEVICES * MSG1, LANES), in_s...  2.61 us
  transfers between devices with their start and end apart: 2, of which 2 were waited for; matrix products, arithmetic and copies ran while one was open for 0% of the time, Pallas kernels for 7%

profile of v6, /device:TPU:1, one launch (start us, length us, event | category | flops | bytes accessed | tf_op | source)
XLA Modules:
  0.0 104.1 jit_solution(10057730480117528050)
XLA Ops:
  0.6 0.0 copy-start.3
  0.7 2.6 %shard_map.120 = f32[2304,128]{1,0:T(8,128)} custom-call(s32[8,128]{1,0:T(8,128)} %bitcast.19, f32[128,1024]{1,0:T(8,128)} %coef_hbm.1, f32[8,128]{1,0:T(8,128)} %bitcast.21, f32[8,128]{1,0:T(8,128)} %bitcast.23, f32[2,128]{1,0:T(2,128)} %bitcast.26), custom_call_target="tpu_custom_call" | custom-call | tf_op jit(solution)/shard_map/pallas_call | solution.py:506
  3.3 11.9 %all-to-all-start = ((f32[128,9,2,128]{3,2,1,0:T(2,128)}), f32[128,9,2,128]{3,2,1,0:T(2,128)}, u32[]{:S(2)}, u32[]{:S(2)}) async-start(f32[128,9,2,128]{3,2,1,0:T(2,128)} %bitcast.30), calls=%async_computation | async-start | bytes 2359296 | tf_op jit(solution)/shard_map/all_to_all | solution.py:467
  15.2 0.0 copy-done.3
  15.2 0.0 copy-done.4
  15.2 5.3 %shard_map.121 = (f32[4,136,512]{2,1,0:T(8,128)}, bf16[3,1024,512]{2,1,0:T(8,128)(2,1)}, bf16[3,1024,512]{2,1,0:T(8,128)(2,1)}) custom-call(f32[1,2048]{1,0:T(1,128)S(1)} %copy-done.3, f32[1,2048]{1,0:T(1,128)S(1)} %copy-done.4), custom_call_target="tpu_custom_call" | custom-call | flops 4194304 | bytes 2097152 | tf_op jit(solution)/shard_map/pallas_call | solution.py:527
  20.5 14.1 %all-to-all-done = f32[128,9,2,128]{3,2,1,0:T(2,128)} async-done(((f32[128,9,2,128]{3,2,1,0:T(2,128)}), f32[128,9,2,128]{3,2,1,0:T(2,128)}, u32[]{:S(2)}, u32[]{:S(2)}) %all-to-all-start) | async-done | bytes 1179680 | tf_op jit(solution)/shard_map/all_to_all | solution.py:467
  34.6 7.3 %shard_map.122 = f32[2,2,4,2,17,8,128]{6,5,4,3,2,1,0:T(8,128)} custom-call(f32[2304,128]{1,0:T(8,128)} %bitcast.5.in_hbm, f32[4,136,512]{2,1,0:T(8,128)} %get-tuple-element.18.base_hbm, bf16[3,1024,512]{2,1,0:T(8,128)(2,1)} %get-tuple-element.19.hi_hbm, bf16[3,1024,512]{2,1,0:T(8,128)(2,1)} %get-tuple-element.20.low_hbm), custom_call_target="tpu_custom_call" | custom-call | tf_op jit(solution)/shard_map/pallas_call | solution.py:558
  41.8 0.0 copy-start
  41.8 0.0 copy-start.5
  41.8 0.0 copy-start.6
  41.9 5.1 %all-to-all-start.1 = ((f32[128,17,2,128]{3,2,1,0:T(2,128)}), f32[128,17,2,128]{3,2,1,0:T(2,128)S(1)}, u32[]{:S(2)}, u32[]{:S(2)}) async-start(f32[128,17,2,128]{3,2,1,0:T(2,128)} %bitcast.29), calls=%async_computation.1 | async-start | bytes 4456448 | tf_op jit(solution)/shard_map/all_to_all | solution.py:467
  47.0 0.0 copy-start.1
  47.0 0.0 copy-start.2
  47.7 0.0 copy-done
  47.7 1.6 %shard_map.123 = (bf16[8,128,256]{2,1,0:T(8,128)(2,1)S(1)}, f32[1]{0:T(128)}) custom-call(s32[8,128]{1,0:T(8,128)S(1)} %bitcast.20, f32[2304,128]{1,0:T(8,128)} %bitcast.5.in_hbm), custom_call_target="tpu_custom_call" | custom-call | flops 2097152 | bytes 2048 | tf_op jit(solution)/shard_map/pallas_call | solution.py:543
  49.3 29.6 %all-to-all-done.1 = f32[128,17,2,128]{3,2,1,0:T(2,128)S(1)} async-done(((f32[128,17,2,128]{3,2,1,0:T(2,128)}), f32[128,17,2,128]{3,2,1,0:T(2,128)S(1)}, u32[]{:S(2)}, u32[]{:S(2)}) %all-to-all-start.1) | async-done | bytes 2228256 | tf_op jit(solution)/shard_map/all_to_all | solution.py:467
  78.9 0.0 copy-done.5
  78.9 2.8 %shard_map.124 = (f32[1024,256]{1,0:T(8,128)S(1)}, f32[192,128]{1,0:T(8,128)S(1)}, f32[2,128]{1,0:T(2,128)S(1)}, f32[1024,256]{1,0:T(8,128)}) custom-call(f32[4352,128]{1,0:T(8,128)S(1)} %bitcast.16, bf16[8,128,256]{2,1,0:T(8,128)(2,1)S(1)} %get-tuple-element.21.choice_ref, f32[2,128]{1,0:T(2,128)S(1)} %bitcast.27, f32[2,128]{1,0:T(2,128)S(1)} %bitcast.28, ...), custom_call_target="tpu_custom_call" | custom-call | tf_op jit(solution)/shard_map/pallas_call | solution.py:569
  81.7 7.5 %all_to_all.20 = f32[8,24,128]{2,1,0:T(8,128)S(1)} all-to-all(f32[8,24,128]{2,1,0:T(8,128)S(1)} %bitcast.18), channel_id=1, replica_groups=mesh['z_lo'=2,'x'=4,'z_hi'=2,'y'=4,'core'=2] {'x','z_lo'}, dimensions={0} | all-to-all | bytes 196608 | tf_op jit(solution)/shard_map/all_to_all | solution.py:467
  89.2 0.0 copy-done.2
  89.2 2.0 %shard_map.125 = (f32[8,128]{1,0:T(8,128)}, f32[32,128]{1,0:T(8,128)S(1)}, f32[2,128]{1,0:T(2,128)S(1)}, f32[1024,256]{1,0:T(8,128)}, f32[1]{0:T(128)}) custom-call(f32[192,128]{1,0:T(8,128)S(1)} %bitcast.17, f32[1024,256]{1,0:T(8,128)S(1)} %get-tuple-element.24.tile_ref, f32[8,128]{1,0:T(8,128)S(1)} %bitcast.22, ...), custom_call_target="tpu_custom_call", output_to_operand_aliasing={{3}: (4, {})} | custom-call | tf_op jit(solution)/shard_map/pallas_call | solution.py:584
  91.2 12.3 %all_to_all.21 = f32[16,2,128]{2,1,0:T(2,128)S(1)} all-to-all(f32[16,2,128]{2,1,0:T(2,128)S(1)} %bitcast.25), channel_id=1, replica_groups=mesh['z_lo'=2,'x'=4,'z_hi'=2,'y'=4,'core'=2] {'core','y','z_hi'}, dimensions={0} | all-to-all | bytes 32768 | tf_op jit(solution)/shard_map/all_to_all | solution.py:467
  103.6 0.6 clamp_bitcast_fusion
  (4 shorter events, 0.0 us)
Async XLA Ops:
  0.6 14.6 %copy-start.3 = (f32[1,2048]{1,0:T(1,128)S(1)}, f32[1,2048]{1,0:T(1,128)}, u32[]{:S(2)}) copy-start(f32[1,2048]{1,0:T(1,128)} %mean_ref.1) | copy-start | bytes 24580
  0.6 14.6 %copy-start.4 = (f32[1,2048]{1,0:T(1,128)S(1)}, f32[1,2048]{1,0:T(1,128)}, u32[]{:S(2)}) copy-start(f32[1,2048]{1,0:T(1,128)} %spread_ref.1) | copy-start | bytes 24580
  3.3 31.3 %all-to-all-start = ((f32[128,9,2,128]{3,2,1,0:T(2,128)}), f32[128,9,2,128]{3,2,1,0:T(2,128)}, u32[]{:S(2)}, u32[]{:S(2)}) async-start(f32[128,9,2,128]{3,2,1,0:T(2,128)} %bitcast.30), calls=%async_computation | async-start | bytes 2359296 | tf_op jit(solution)/shard_map/all_to_all | solution.py:467
  41.8 5.9 %copy-start = (s32[1024,1]{0,1:T(1,128)S(1)}, s32[1024,1]{0,1:T(1,128)}, u32[]{:S(2)}) copy-start(s32[1024,1]{0,1:T(1,128)} %param.10) | copy-start | bytes 12292
  41.8 37.1 %copy-start.5 = (f32[256]{0:T(256)S(1)}, f32[256]{0:T(256)}, u32[]{:S(2)}) copy-start(f32[256]{0:T(256)} %param.16) | copy-start | bytes 3076
  41.8 37.0 %copy-start.6 = (f32[256]{0:T(256)S(1)}, f32[256]{0:T(256)}, u32[]{:S(2)}) copy-start(f32[256]{0:T(256)} %param.15) | copy-start | bytes 3076
  41.9 37.0 %all-to-all-start.1 = ((f32[128,17,2,128]{3,2,1,0:T(2,128)}), f32[128,17,2,128]{3,2,1,0:T(2,128)S(1)}, u32[]{:S(2)}, u32[]{:S(2)}) async-start(f32[128,17,2,128]{3,2,1,0:T(2,128)} %bitcast.29), calls=%async_computation.1 | async-start | bytes 4456448 | tf_op jit(solution)/shard_map/all_to_all | solution.py:467
  47.0 42.2 %copy-start.1 = (f32[1024]{0:T(1024)S(1)}, f32[1024]{0:T(1024)}, u32[]{:S(2)}) copy-start(f32[1024]{0:T(1024)} %param.13) | copy-start | bytes 12292
  47.0 42.2 %copy-start.2 = (f32[1024]{0:T(1024)S(1)}, f32[1024]{0:T(1024)}, u32[]{:S(2)}) copy-start(f32[1024]{0:T(1024)} %param.14) | copy-start | bytes 12292
